TPU v7x, 32 devices: a whole 2x2x4 slice. The times are simulated.
32 devices in a mesh: dp: 8 (over z, x), ctx: 4 (over y, core).
Axes of the slice: x: 2, y: 2, z: 4, core: 2. Of those that a mesh axis runs over, the one named last changes fastest.
Arguments:
- query: bfloat16 [16, 256, 4096], P('dp', 'ctx'), may hold values from -6 to 6
- key_in: bfloat16 [16, 256, 1024], P('dp', 'ctx'), may hold values from -6 to 6
- value_in: bfloat16 [16, 256, 1024], P('dp', 'ctx'), may hold values from -6 to 6
- out_grad: bfloat16 [16, 256, 4096], P('dp', 'ctx'), may hold values from -1.5 to 1.5
- masked: int32 [16, 128], P('dp'), may hold values from 0 to 255, as said below
- bucket: int32 [16, 256], P('dp', 'ctx'), may hold values from 0 to 15
Outputs:
- query_grad: bfloat16 [16, 256, 4096], P('dp', 'ctx')
- key_grad: bfloat16 [16, 256, 1024], P('dp', 'ctx')
- value_grad: bfloat16 [16, 256, 1024], P('dp', 'ctx')
- bias_query_grad: float32 [4, 1024], P('ctx', 'dp')
- bias_kv_grad: float32 [2, 1024], P(None, 'dp')
Inputs may be any that keep to these rules, and one draw needn't show every extreme that they name: Each document has exactly 128 distinct masked positions.
All inputs are finite; a program needn't handle non-finite values.
Results may differ from a plain program's by a relative error of at most 0.012.
The roundings to bfloat16 on the way count: a program that leaves them out, or rounds other values in their place, can miss the bound.
Values may be sent and summed in bfloat16 or wider, within the bound.
No kernel may reach another device: no remote copies, remote signals or barrier semaphores. Data moves between devices by JAX's collectives and lax.ppermute only.
A program may use at most 64 MiB of HBM per device.

v0:
```python
import math

import jax
import jax.numpy as jnp
from jax import lax
from jax.sharding import PartitionSpec as P

H = 32
KVH = 8
HD = 128
NB = 16


def carried_in(value, axis, combine, identity):
    length, place = (lax.axis_size(axis), lax.axis_index(axis))
    everything = jax.tree.map(lambda part: lax.all_gather(part, axis), value)
    start = jax.tree.map(
        lambda part, zero: jnp.broadcast_to(jnp.asarray(zero, part.dtype), part.shape),
        value,
        identity,
    )

    def lap(k, before):
        reached = k < place
        new = combine(before, jax.tree.map(lambda part: part[k], everything))
        return jax.tree.map(lambda a, b: jnp.where(reached, a, b), new, before)

    return lax.fori_loop(0, length, lap, start)


def from_root(value, axis, source):
    kept = jnp.where(lax.axis_index(axis) == source, value, 0).astype(value.dtype)
    return lax.psum(kept, axis)


def softmax_rows(scores):
    shifted = scores - jnp.max(scores, axis=-1, keepdims=True)
    exponent = jnp.exp(shifted)
    return exponent / jnp.sum(exponent, axis=-1, keepdims=True)


def head_pass(inputs):
    query_one, key_one, value_one, cot_one = inputs
    inv_root = 1.0 / math.sqrt(HD)
    scores = (
        jnp.einsum("qd,kd->qk", query_one, key_one, preferred_element_type=jnp.float32) * inv_root
    )
    attn_probs = softmax_rows(scores)
    probs_low = attn_probs.astype(jnp.bfloat16)
    attn_out = jnp.einsum("qk,kd->qd", probs_low, value_one, preferred_element_type=jnp.float32)
    delta_rows = jnp.sum(cot_one.astype(jnp.float32) * attn_out, axis=-1)
    value_full = jnp.einsum("qk,qd->kd", probs_low, cot_one, preferred_element_type=jnp.float32)
    prob_grad = jnp.einsum("qd,kd->qk", cot_one, value_one, preferred_element_type=jnp.float32)
    score_low = (attn_probs * (prob_grad - delta_rows[:, None]) * inv_root).astype(jnp.bfloat16)
    query_full = jnp.einsum("qk,kd->qd", score_low, key_one, preferred_element_type=jnp.float32)
    key_full = jnp.einsum("qk,qd->kd", score_low, query_one, preferred_element_type=jnp.float32)
    return (query_full, key_full, value_full)


def to_items(array, count):
    docs_here, length = (array.shape[0], array.shape[1])
    return (
        array.reshape(docs_here, length, count, HD)
        .transpose(0, 2, 1, 3)
        .reshape(docs_here * count, length, HD)
    )


def attend_heads(query_here, key_here, value_here, cot_here, heads_dev, slots_dev):
    docs_here, length = (query_here.shape[0], query_here.shape[1])
    per_slot = heads_dev // slots_dev

    def widen(array):
        shaped = array.reshape(docs_here, length, slots_dev, HD).transpose(0, 2, 1, 3)
        return jnp.repeat(shaped, per_slot, axis=1).reshape(docs_here * heads_dev, length, HD)

    query_full, key_full, value_full = lax.map(
        head_pass,
        (
            to_items(query_here, heads_dev),
            widen(key_here),
            widen(value_here),
            to_items(cot_here, heads_dev),
        ),
    )
    query_sums = jnp.sum(jnp.sum(query_full, axis=1).reshape(docs_here, heads_dev * HD), axis=0)
    query_back = query_full.astype(jnp.bfloat16).reshape(docs_here, heads_dev, length, HD)
    query_back = query_back.transpose(0, 2, 1, 3).reshape(docs_here, length, heads_dev * HD)

    def slot_rows(grads):
        merged = jnp.sum(grads.reshape(docs_here, slots_dev, per_slot, length, HD), axis=2)
        return merged.transpose(0, 2, 1, 3).reshape(docs_here, length, slots_dev * HD)

    return (query_back, slot_rows(key_full), slot_rows(value_full), query_sums)


def add_pairs(earlier, later):
    return (earlier[0] + later[0], earlier[1] + later[1])


def per_device(query, key_in, value_in, out_grad, masked, bucket):
    n_ctx = lax.axis_size("ctx")
    n_dp = lax.axis_size("dp")
    docs_dev, tok_count = (query.shape[0], query.shape[1])
    length = tok_count * n_ctx
    heads_dev = H // n_ctx
    positions = lax.axis_index("ctx") * tok_count + jnp.arange(tok_count, dtype=jnp.int32)
    is_masked = jnp.any(masked[:, None, :] == positions[None, :, None], axis=-1)
    loss_weight = is_masked.astype(jnp.float32) * NB / (bucket.astype(jnp.float32) + 1.0)
    cotangent = (out_grad.astype(jnp.float32) * loss_weight[:, :, None]).astype(jnp.bfloat16)
    key_heads = key_in.reshape(docs_dev, tok_count, KVH, HD)
    value_heads = value_in.reshape(docs_dev, tok_count, KVH, HD)
    slot_total = max(KVH, n_ctx)
    copies = slot_total // KVH
    key_copies = jnp.repeat(key_heads, copies, axis=2).reshape(docs_dev, tok_count, slot_total * HD)
    value_copies = jnp.repeat(value_heads, copies, axis=2).reshape(
        docs_dev, tok_count, slot_total * HD
    )
    query_here, cot_here, key_here, value_here = (
        lax.all_to_all(query, "ctx", split_axis=2, concat_axis=1, tiled=True),
        lax.all_to_all(cotangent, "ctx", split_axis=2, concat_axis=1, tiled=True),
        lax.all_to_all(key_copies, "ctx", split_axis=2, concat_axis=1, tiled=True),
        lax.all_to_all(value_copies, "ctx", split_axis=2, concat_axis=1, tiled=True),
    )
    query_back, key_terms, value_terms, query_sums = attend_heads(
        query_here, key_here, value_here, cot_here, heads_dev, slot_total // n_ctx
    )
    key_rows, value_rows = (
        lax.all_to_all(
            key_terms.astype(jnp.bfloat16), "ctx", split_axis=1, concat_axis=2, tiled=True
        ).astype(key_terms.dtype),
        lax.all_to_all(
            value_terms.astype(jnp.bfloat16), "ctx", split_axis=1, concat_axis=2, tiled=True
        ).astype(value_terms.dtype),
    )
    query_grad = lax.all_to_all(query_back, "ctx", split_axis=1, concat_axis=2, tiled=True)
    key_full = jnp.sum(key_rows.reshape(docs_dev, tok_count, KVH, copies, HD), axis=3).reshape(
        docs_dev, tok_count, KVH * HD
    )
    value_full = jnp.sum(value_rows.reshape(docs_dev, tok_count, KVH, copies, HD), axis=3).reshape(
        docs_dev, tok_count, KVH * HD
    )
    pair_local = jnp.stack([jnp.sum(key_full, axis=(0, 1)), jnp.sum(value_full, axis=(0, 1))])
    pair_group = lax.psum(pair_local, "ctx")
    lower_terms = carried_in(
        (query_sums, pair_group),
        "dp",
        add_pairs,
        (jnp.zeros_like(query_sums), jnp.zeros_like(pair_group)),
    )
    running = add_pairs(lower_terms, (query_sums, pair_group))
    query_total, pair_total = (
        from_root(running[0], "dp", n_dp - 1),
        from_root(running[1], "dp", n_dp - 1),
    )
    norm_factor = 1.0 / math.sqrt(docs_dev * n_dp * length)
    dp_index = lax.axis_index("dp")
    query_width = query_total.shape[0] // n_dp
    pair_width = pair_total.shape[1] // n_dp
    query_piece = lax.dynamic_slice_in_dim(query_total, dp_index * query_width, query_width, 0)
    pair_piece = lax.dynamic_slice_in_dim(pair_total, dp_index * pair_width, pair_width, 1)
    return (
        query_grad,
        key_full.astype(jnp.bfloat16),
        value_full.astype(jnp.bfloat16),
        (query_piece * norm_factor).reshape(1, query_width),
        pair_piece * norm_factor,
    )


def solution(mesh):
    in_specs = (
        P("dp", "ctx", None),
        P("dp", "ctx", None),
        P("dp", "ctx", None),
        P("dp", "ctx", None),
        P("dp", None),
        P("dp", "ctx"),
    )
    out_specs = (
        P("dp", "ctx", None),
        P("dp", "ctx", None),
        P("dp", "ctx", None),
        P("ctx", "dp"),
        P(None, "dp"),
    )
    return jax.shard_map(
        per_device, mesh=mesh, in_specs=in_specs, out_specs=out_specs, check_vma=False
    )
```

profile of v0, /device:TPU:0, one launch (start us, length us, event | category | flops | bytes accessed | tf_op | source)
XLA Modules:
  0.0 303.5 jit_solution(11567495984905517460)
XLA Ops:
  0.7 1.4 copy.97
  2.0 1.1 reshape.98
  3.1 4.3 %all-to-all-start.1 = ((bf16[4,2,16384]{2,1,0:T(2,128)(2,1)}), bf16[4,2,16384]{2,1,0:T(2,128)(2,1)S(1)}, u32[]{:S(2)}, u32[]{:S(2)}) async-start(bf16[4,2,16384]{2,1,0:T(2,128)(2,1)} %reshape.98), calls=%async_computation.1 | async-start | bytes 524288 | tf_op jit(solution)/shard_map/all_to_all | solution.py:122
  7.8 1.1 reshape.102
  9.1 4.3 %all-to-all-done.1 = bf16[4,2,16384]{2,1,0:T(2,128)(2,1)S(1)} async-done(((bf16[4,2,16384]{2,1,0:T(2,128)(2,1)}), bf16[4,2,16384]{2,1,0:T(2,128)(2,1)S(1)}, u32[]{:S(2)}, u32[]{:S(2)}) %all-to-all-start.1) | async-done | bytes 262176 | tf_op jit(solution)/shard_map/all_to_all | solution.py:122
  13.4 4.0 %all-to-all-start.3 = ((bf16[4,2,16384]{2,1,0:T(2,128)(2,1)}), bf16[4,2,16384]{2,1,0:T(2,128)(2,1)}, u32[]{:S(2)}, u32[]{:S(2)}) async-start(bf16[4,2,16384]{2,1,0:T(2,128)(2,1)} %reshape.102), calls=%async_computation.3 | async-start | bytes 524288 | tf_op jit(solution)/shard_map/all_to_all | solution.py:123
  17.7 2.8 copy.100
  20.6 2.7 reshape.100
  23.5 3.5 %all-to-all-start.2 = ((bf16[4,2,65536]{2,1,0:T(2,128)(2,1)}), bf16[4,2,65536]{2,1,0:T(2,128)(2,1)S(1)}, u32[]{:S(2)}, u32[]{:S(2)}) async-start(bf16[4,2,65536]{2,1,0:T(2,128)(2,1)} %reshape.100), calls=%async_computation.2 | async-start | bytes 2097152 | tf_op jit(solution)/shard_map/all_to_all | solution.py:121
  27.0 5.0 %copy.94 = bf16[2,64,4096]{1,0,2:T(2,128)(2,1)S(1)} copy(bf16[2,64,4096]{2,1,0:T(8,128)(2,1)} %param.10) | data formatting | bytes 2097152 | tf_op args[0]
  32.1 2.7 reshape.96
  34.8 6.7 %all-to-all-done.2 = bf16[4,2,65536]{2,1,0:T(2,128)(2,1)S(1)} async-done(((bf16[4,2,65536]{2,1,0:T(2,128)(2,1)}), bf16[4,2,65536]{2,1,0:T(2,128)(2,1)S(1)}, u32[]{:S(2)}, u32[]{:S(2)}) %all-to-all-start.2) | async-done | bytes 1048608 | tf_op jit(solution)/shard_map/all_to_all | solution.py:121
  41.4 3.5 %all-to-all-start = ((bf16[4,2,65536]{2,1,0:T(2,128)(2,1)}), bf16[4,2,65536]{2,1,0:T(2,128)(2,1)S(1)}, u32[]{:S(2)}, u32[]{:S(2)}) async-start(bf16[4,2,65536]{2,1,0:T(2,128)(2,1)} %reshape.96), calls=%async_computation | async-start | bytes 2097152 | tf_op jit(solution)/shard_map/all_to_all | solution.py:120
  45.9 1.3 reshape.103
  48.4 3.1 %reshape.101 = bf16[4096,2,64]{2,1,0:T(2,128)(2,1)S(1)} reshape(bf16[4,2,65536]{2,1,0:T(2,128)(2,1)} %copy-done) | data formatting | bytes 2097152
  51.5 3.6 %copy.101 = bf16[2,64,4,1024]{3,1,2,0:T(8,128)(2,1)} copy(bf16[2,64,4,1024]{1,0,3,2:T(2,128)(2,1)S(1)} %bitcast.162) | data formatting | bytes 2097152 | tf_op jit(solution)/shard_map/all_to_all | solution.py:121
  55.1 1.5 copy.125
  56.6 1.2 copy.102
  57.8 1.5 all-to-all-done
  59.4 1.4 reshape.97
  60.8 1.5 copy.95
  63.8 94.7 %while.30 = (s32[]{:T(128)}, f32[16,256,128]{2,1,0:T(8,128)}, f32[16,256,128]{2,1,0:T(8,128)}, f32[16,256,128]{2,1,0:T(8,128)}, bf16[16,256,128]{2,1,0:T(8,128)(...) while((s32[]{:T(128)}, f32[16,256,128]{2,1,0:T(8,128)}, ...), condition=%wide.region_5.6_spmd, body=%wide.region_1.5_spmd.sunk | while | flops 101809408 | bytes 2965605 | solution.py:77
  64.1 1.7 fusion.68
  67.0 1.0 fusion.65
  70.0 1.7 fusion.68
  72.9 1.0 fusion.65
  75.9 1.7 fusion.68
  78.8 1.0 fusion.65
  81.8 1.7 fusion.68
  84.7 1.0 fusion.65
  87.8 1.7 fusion.68
  90.6 1.0 fusion.65
  93.7 1.7 fusion.68
  96.5 1.0 fusion.65
  99.6 1.7 fusion.68
  102.5 1.0 fusion.65
  105.5 1.7 fusion.68
  108.4 1.0 fusion.65
  111.4 1.7 fusion.68
  114.3 1.0 fusion.65
  117.3 1.7 fusion.68
  120.2 1.0 fusion.65
  123.3 1.7 fusion.68
  126.1 1.0 fusion.65
  129.2 1.7 fusion.68
  132.1 1.0 fusion.65
  135.1 1.7 fusion.68
  138.0 1.0 fusion.65
  141.0 1.7 fusion.68
  143.9 1.0 fusion.65
  146.9 1.7 fusion.68
  152.8 1.7 fusion.68
  158.5 2.7 bitcast_reduce_fusion
  162.2 3.4 %all-to-all-start.5 = ((bf16[2,256,256]{2,0,1:T(2,128)(2,1)}), bf16[2,256,256]{2,0,1:T(2,128)(2,1)S(1)}, u32[]{:S(2)}, u32[]{:S(2)}) async-start(bf16[2,256,256]{2,0,1:T(2,128)(2,1)} %copy.112), calls=%async_computation.5 | async-start | bytes 524288 | tf_op jit(solution)/shard_map/all_to_all | solution.py:129
  166.6 4.9 %all-to-all-done.5 = bf16[2,256,256]{2,0,1:T(2,128)(2,1)S(1)} async-done(((bf16[2,256,256]{2,0,1:T(2,128)(2,1)}), bf16[2,256,256]{2,0,1:T(2,128)(2,1)S(1)}, u32[]{:S(2)}, u32[]{:S(2)}) %all-to-all-start.5) | async-done | bytes 262176 | tf_op jit(solution)/shard_map/all_to_all | solution.py:129
  171.6 3.4 %all-to-all-start.6 = ((bf16[2,256,256]{2,0,1:T(2,128)(2,1)}), bf16[2,256,256]{2,0,1:T(2,128)(2,1)S(1)}, u32[]{:S(2)}, u32[]{:S(2)}) async-start(bf16[2,256,256]{2,0,1:T(2,128)(2,1)} %copy.116), calls=%async_computation.6 | async-start | bytes 524288 | tf_op jit(solution)/shard_map/all_to_all | solution.py:132
  175.0 2.5 fusion.32
  177.5 31.6 %all-gather = f32[8192]{0:T(1024)S(1)} all-gather(f32[1024]{0:T(1024)S(1)} %reduce_sum.83), channel_id=2, replica_groups=mesh['dp'=8,'ctx'=4] {'dp'}, dimensions={0}, use_global_device_ids=true | all-gather | bytes 36864 | tf_op jit(solution)/shard_map/all_gather | solution.py:16
  209.6 2.1 copy.108
  211.8 3.5 %all-to-all-start.4 = ((bf16[2,256,1024]{2,0,1:T(2,128)(2,1)}), bf16[2,256,1024]{2,0,1:T(2,128)(2,1)S(1)}, u32[]{:S(2)}, u32[]{:S(2)}) async-start(bf16[2,256,1024]{2,0,1:T(2,128)(2,1)} %copy.108), calls=%async_computation.4 | async-start | bytes 2097152 | tf_op jit(solution)/shard_map/all_to_all | solution.py:136
  215.5 15.8 %psum.21 = f32[2,1024]{1,0:T(2,128)S(1)} all-reduce(f32[2,1024]{1,0:T(2,128)S(1)} %pad_maximum_fusion), channel_id=1, replica_groups=mesh['dp'=8,'ctx'=4] {'ctx'}, use_global_device_ids=true, to_apply=%region_12.13 | all-reduce | flops 2048 | bytes 16384 | tf_op jit(solution)/shard_map/psum | solution.py:144
  231.3 30.5 %all-gather.2 = f32[8,2,1024]{2,1,0:T(2,128)S(1)} all-gather(f32[1,2,1024]{2,1,0:T(2,128)S(1)} %bitcast.195), channel_id=3, replica_groups=mesh['dp'=8,'ctx'=4] {'dp'}, dimensions={0}, use_global_device_ids=true | all-gather | bytes 73728 | tf_op jit(solution)/shard_map/all_gather | solution.py:16
  264.0 37.0 %all-reduce = (f32[1024]{0:T(1024)S(1)}, f32[2,1024]{1,0:T(2,128)S(1)}) all-reduce(f32[1024]{0:T(1024)S(1)} %add_select_fusion.3, f32[2,1024]{1,0:T(2,128)S(1)} %add_select_fusion.2), channel_id=1, replica_groups=mesh['dp'=8,'ctx'=4] {'dp'}, use_global_device_ids=true, to_apply=%region_15.16 | all-reduce | flops 3072 | bytes 24576 | tf_op jit(solution)/shard_map/psum | solution.py:33
  302.4 1.1 copy.121
  (199 shorter events, 64.4 us)
Async XLA Ops:
  0.6 6.8 %copy-start.3 = (bf16[2,64,1024]{2,1,0:T(8,128)(2,1)S(1)}, bf16[2,64,1024]{2,1,0:T(8,128)(2,1)}, u32[]{:S(2)}) copy-start(bf16[2,64,1024]{2,1,0:T(8,128)(2,1)} %param.12) | copy-start | bytes 786436
  0.6 8.3 %copy-start.4 = (s32[2,128]{1,0:T(2,128)S(1)}, s32[2,128]{1,0:T(2,128)}, u32[]{:S(2)}) copy-start(s32[2,128]{1,0:T(2,128)} %param.14) | copy-start | bytes 3076
  0.7 8.4 %copy-start.5 = (s32[2,64]{1,0:T(2,128)S(1)}, s32[2,64]{1,0:T(2,128)}, u32[]{:S(2)}) copy-start(s32[2,64]{1,0:T(2,128)} %param.15) | copy-start | bytes 1540
  0.7 16.8 %copy-start.2 = (bf16[2,64,4096]{2,1,0:T(8,128)(2,1)S(1)}, bf16[2,64,4096]{2,1,0:T(8,128)(2,1)}, u32[]{:S(2)}) copy-start(bf16[2,64,4096]{2,1,0:T(8,128)(2,1)} %param.13) | copy-start | bytes 3145732
  3.1 10.3 %all-to-all-start.1 = ((bf16[4,2,16384]{2,1,0:T(2,128)(2,1)}), bf16[4,2,16384]{2,1,0:T(2,128)(2,1)S(1)}, u32[]{:S(2)}, u32[]{:S(2)}) async-start(bf16[4,2,16384]{2,1,0:T(2,128)(2,1)} %reshape.98), calls=%async_computation.1 | async-start | bytes 524288 | tf_op jit(solution)/shard_map/all_to_all | solution.py:122
  13.4 10.1 %all-to-all-start.3 = ((bf16[4,2,16384]{2,1,0:T(2,128)(2,1)}), bf16[4,2,16384]{2,1,0:T(2,128)(2,1)}, u32[]{:S(2)}, u32[]{:S(2)}) async-start(bf16[4,2,16384]{2,1,0:T(2,128)(2,1)} %reshape.102), calls=%async_computation.3 | async-start | bytes 524288 | tf_op jit(solution)/shard_map/all_to_all | solution.py:123
  23.5 17.9 %all-to-all-start.2 = ((bf16[4,2,65536]{2,1,0:T(2,128)(2,1)}), bf16[4,2,65536]{2,1,0:T(2,128)(2,1)S(1)}, u32[]{:S(2)}, u32[]{:S(2)}) async-start(bf16[4,2,65536]{2,1,0:T(2,128)(2,1)} %reshape.100), calls=%async_computation.2 | async-start | bytes 2097152 | tf_op jit(solution)/shard_map/all_to_all | solution.py:121
  41.4 6.2 %copy-start = (bf16[4,2,65536]{2,1,0:T(2,128)(2,1)}, bf16[4,2,65536]{2,1,0:T(2,128)(2,1)S(1)}, u32[]{:S(2)}) copy-start(bf16[4,2,65536]{2,1,0:T(2,128)(2,1)S(1)} %all-to-all-done.2) | copy-start | bytes 3145732
  41.4 17.9 %all-to-all-start = ((bf16[4,2,65536]{2,1,0:T(2,128)(2,1)}), bf16[4,2,65536]{2,1,0:T(2,128)(2,1)S(1)}, u32[]{:S(2)}, u32[]{:S(2)}) async-start(bf16[4,2,65536]{2,1,0:T(2,128)(2,1)} %reshape.96), calls=%async_computation | async-start | bytes 2097152 | tf_op jit(solution)/shard_map/all_to_all | solution.py:120
  62.6 1.0 copy-start.1
  162.2 9.4 %all-to-all-start.5 = ((bf16[2,256,256]{2,0,1:T(2,128)(2,1)}), bf16[2,256,256]{2,0,1:T(2,128)(2,1)S(1)}, u32[]{:S(2)}, u32[]{:S(2)}) async-start(bf16[2,256,256]{2,0,1:T(2,128)(2,1)} %copy.112), calls=%async_computation.5 | async-start | bytes 524288 | tf_op jit(solution)/shard_map/all_to_all | solution.py:129
  171.6 40.2 %all-to-all-start.6 = ((bf16[2,256,256]{2,0,1:T(2,128)(2,1)}), bf16[2,256,256]{2,0,1:T(2,128)(2,1)S(1)}, u32[]{:S(2)}, u32[]{:S(2)}) async-start(bf16[2,256,256]{2,0,1:T(2,128)(2,1)} %copy.116), calls=%async_computation.6 | async-start | bytes 524288 | tf_op jit(solution)/shard_map/all_to_all | solution.py:132
  211.8 90.3 %all-to-all-start.4 = ((bf16[2,256,1024]{2,0,1:T(2,128)(2,1)}), bf16[2,256,1024]{2,0,1:T(2,128)(2,1)S(1)}, u32[]{:S(2)}, u32[]{:S(2)}) async-start(bf16[2,256,1024]{2,0,1:T(2,128)(2,1)} %copy.108), calls=%async_computation.4 | async-start | bytes 2097152 | tf_op jit(solution)/shard_map/all_to_all | solution.py:136
where the time goes:
time: 307 us; the launch traced here: 303 us
  blocking collectives  115 us (37%)
  matrix products  78 us (25%)
  local copies, waits for them, and re-layouts  57.1 us (19%)
  starting transfers between devices  25.7 us (8%)
  waiting for transfers between devices  17.7 us (6%)
  other arithmetic  8.25 us (3%)
    all_gather x2, blocking collectives, carried_in(): everything = jax.tree.map(lambda part: lax.all_gather(part, axis), value)  62.1 us
    psum x1, blocking collectives, from_root(): return lax.psum(kept, axis)  37 us
    dot_general x16, matrix products, head_pass(): jnp.einsum('qk,qd->kd', probs_low, cot_one, preferred_element_type=jnp.fl...  26.7 us
    unnamed x27, local copies, waits for them, and re-layouts  22.8 us
    dot_general x16, matrix products, head_pass(): jnp.einsum('qd,kd->qk', cot_one, value_one, preferred_element_type=jnp.fl...  16.6 us
    psum x1, blocking collectives, per_device(): pair_group = lax.psum(pair_local, 'ctx')  15.8 us
    dynamic_slice x32, local copies, waits for them, and re-layouts, attend_heads(): lax.map(head_pass, (to_items(query_here, heads_dev), widen(key_here), wid...  15.2 us
    dot_general x16, matrix products, head_pass(): jnp.einsum('qk,kd->qd', score_low, key_one, preferred_element_type=jnp.fl...  14 us
  transfers between devices with their start and end apart: 7, of which 5 were waited for; matrix products, arithmetic and copies ran while one was open for 12% of the time, Pallas kernels for 0%

commit v1 on v0

v1 whole, which is shorter than its diff:
```python
import functools
import math

import jax
import jax.numpy as jnp
from jax import lax
from jax.experimental import pallas as pl
from jax.experimental.pallas import tpu as pltpu
from jax.sharding import PartitionSpec as P

H = 32
KVH = 8
HD = 128
NB = 16
GROUP = H // KVH
STEP = 2

NT = (((1,), (1,)), ((), ()))
NN = (((1,), (0,)), ((), ()))
TN = (((0,), (0,)), ((), ()))


def dot(a, b, dims):
    return lax.dot_general(a, b, dims, preferred_element_type=jnp.float32)


def attend_kernel(n_pieces, tok, step, doc, n_ctx, *refs):
    place_ref, masked_ref, bucket_ref, query_ref, grad_ref = refs[:5]
    piece_refs = refs[5 : 5 + 2 * n_pieces]
    (dq_ref, near_ref, far_ref, qsum_ref, ksum_ref, vsum_ref, weight_ref) = refs[5 + 2 * n_pieces :]
    inv_root = 1.0 / math.sqrt(HD)

    @pl.when(pl.program_id(0) == 0)
    def _():
        rows = lax.broadcasted_iota(jnp.int32, (tok, masked_ref.shape[1]), 0) + place_ref[0] * tok
        hit = jnp.where(masked_ref[doc : doc + 1, :] == rows, 1.0, 0.0)
        is_masked = jnp.max(hit, axis=1, keepdims=True)
        lane = lax.broadcasted_iota(jnp.int32, (tok, tok), 1)
        line = lax.broadcasted_iota(jnp.int32, (tok, tok), 0)
        spread = jnp.where(lane == line, bucket_ref[doc : doc + 1, :].astype(jnp.float32), 0.0)
        level = jnp.sum(spread, axis=1, keepdims=True)
        weight_ref[...] = jnp.broadcast_to(is_masked * NB / (level + 1.0), weight_ref.shape)

    weight = weight_ref[...]
    for s in range(step):
        cols = [slice((s * GROUP + h) * HD, (s * GROUP + h + 1) * HD) for h in range(GROUP)]
        kv = slice(s * HD, (s + 1) * HD)
        q4 = jnp.concatenate([query_ref[0, :, c] for c in cols], axis=0)
        c4 = jnp.concatenate(
            [(grad_ref[0, :, c].astype(jnp.float32) * weight).astype(jnp.bfloat16) for c in cols],
            axis=0,
        )
        keys = jnp.concatenate([r[:, kv] for r in piece_refs[0::2]], axis=0)
        values = jnp.concatenate([r[:, kv] for r in piece_refs[1::2]], axis=0)
        scores = dot(keys, q4, NT)
        prob_grad = dot(values, c4, NT)
        top = jnp.max(scores, axis=0, keepdims=True)
        expo = jnp.exp((scores - top) * inv_root)
        probs = expo * (1.0 / jnp.sum(expo, axis=0, keepdims=True))
        low = probs.astype(jnp.bfloat16)
        delta = jnp.sum(low.astype(jnp.float32) * prob_grad, axis=0, keepdims=True)
        score_low = (probs * (prob_grad - delta) * inv_root).astype(jnp.bfloat16)
        dv = dot(low, c4, NN)
        dk = dot(score_low, q4, NN)
        dq = dot(score_low, keys, TN)
        for h, c in enumerate(cols):
            part = dq[h * tok : (h + 1) * tok]
            dq_ref[0, :, c] = part.astype(jnp.bfloat16)
            qsum_ref[:, c] = jnp.sum(part, axis=0, keepdims=True)
        ksum_ref[:, kv] = jnp.sum(dk, axis=0, keepdims=True)
        vsum_ref[:, kv] = jnp.sum(dv, axis=0, keepdims=True)
        for which, full in ((0, dk), (1, dv)):
            for piece in range(n_pieces):
                part = full[piece * tok : (piece + 1) * tok]
                if piece % 2:
                    far_ref[piece // 2, which, :, kv] = part.astype(jnp.bfloat16)
                else:
                    near_ref[piece // 2, which, :, kv] = part


def attend(place, masked, bucket, query, out_grad, pieces, doc, n_ctx):
    docs, tok, width = query.shape
    kv_width = KVH * HD
    n_pieces = len(pieces)
    step = STEP
    steps = KVH // step
    qw, kw = step * GROUP * HD, step * HD
    half = n_pieces // 2
    piece_specs, piece_args = [], []
    for piece in pieces:
        piece_specs += [
            pl.BlockSpec((tok, kw), lambda g: (0, g)),
            pl.BlockSpec((tok, kw), lambda g: (0, g + steps)),
        ]
        piece_args += [piece, piece]
    wide = pl.BlockSpec((1, tok, qw), lambda g: (doc, 0, g))
    return pl.pallas_call(
        functools.partial(attend_kernel, n_pieces, tok, step, doc, n_ctx),
        grid=(steps,),
        in_specs=[
            pl.BlockSpec(memory_space=pltpu.SMEM),
            pl.BlockSpec(masked.shape, lambda g: (0, 0)),
            pl.BlockSpec(bucket.shape, lambda g: (0, 0)),
            wide,
            wide,
            *piece_specs,
        ],
        out_specs=[
            pl.BlockSpec((1, tok, qw), lambda g: (0, 0, g)),
            pl.BlockSpec((half, 2, tok, kw), lambda g: (0, 0, 0, g)),
            pl.BlockSpec((half, 2, tok, kw), lambda g: (0, 0, 0, g)),
            pl.BlockSpec((1, qw), lambda g: (0, g)),
            pl.BlockSpec((1, kw), lambda g: (0, g)),
            pl.BlockSpec((1, kw), lambda g: (0, g)),
        ],
        out_shape=[
            jax.ShapeDtypeStruct((1, tok, width), jnp.bfloat16),
            jax.ShapeDtypeStruct((half, 2, tok, kv_width), jnp.float32),
            jax.ShapeDtypeStruct((half, 2, tok, kv_width), jnp.bfloat16),
            jax.ShapeDtypeStruct((1, width), jnp.float32),
            jax.ShapeDtypeStruct((1, kv_width), jnp.float32),
            jax.ShapeDtypeStruct((1, kv_width), jnp.float32),
        ],
        scratch_shapes=[pltpu.VMEM((tok, HD), jnp.float32)],
        name="attend",
    )(place, masked, bucket, query, out_grad, *piece_args)


def per_device(query, key_in, value_in, out_grad, masked, bucket):
    n_ctx = lax.axis_size("ctx")
    n_dp = lax.axis_size("dp")
    docs, tok = query.shape[:2]
    chips = n_ctx // 2
    place = lax.axis_index("ctx").astype(jnp.int32).reshape(1)

    def to_sibling(array):
        return lax.ppermute(array, "ctx", [(i, i ^ 1) for i in range(n_ctx)])

    def shift(array, by):
        return lax.ppermute(array, "ctx", [(i, (i + 2 * by) % n_ctx) for i in range(n_ctx)])

    packed = [jnp.concatenate([key_in[d], value_in[d]], axis=-1) for d in range(docs)]
    away = [[shift(packed[d], s) for s in range(1, chips)] for d in range(docs)]
    query_grads, near, far, qsum, ksum, vsum = [], [], [], 0.0, 0.0, 0.0
    for d in range(docs):
        pieces = [packed[d], to_sibling(packed[d])]
        for other in away[d]:
            pieces += [other, to_sibling(other)]
        dq, here, there, qs, ks, vs = attend(
            place, masked, bucket, query, out_grad, pieces, d, n_ctx
        )
        query_grads.append(dq)
        near.append(here)
        far.append(there)
        qsum, ksum, vsum = (qsum + qs, ksum + ks, vsum + vs)

    grads = []
    for d in range(docs):
        back = to_sibling(far[d])
        total = near[d][0] + back[0].astype(jnp.float32)
        for s in range(1, chips):
            sent = (near[d][s] + back[s].astype(jnp.float32)).astype(jnp.bfloat16)
            total = total + shift(sent, -s).astype(jnp.float32)
        grads.append(total.astype(jnp.bfloat16))
    key_grad = jnp.stack([g[0] for g in grads])
    value_grad = jnp.stack([g[1] for g in grads])

    q_w = H * HD // (n_ctx * n_dp)
    p_w = KVH * HD // n_dp
    q_part = qsum.reshape(n_ctx, n_dp, q_w).transpose(1, 0, 2)
    pair = jnp.stack([ksum.reshape(n_dp, p_w), vsum.reshape(n_dp, p_w)], axis=1)
    pair = jnp.broadcast_to(pair.reshape(n_dp, 1, 2 * p_w), (n_dp, n_ctx, 2 * p_w))
    sends = jnp.concatenate([q_part, pair], axis=-1).reshape(n_dp * n_ctx, q_w + 2 * p_w)
    sums = jnp.sum(lax.all_to_all(sends, ("dp", "ctx"), 0, 0), axis=0)
    norm_factor = 1.0 / math.sqrt(docs * n_dp * tok * n_ctx)
    return (
        jnp.concatenate(query_grads, axis=0),
        key_grad,
        value_grad,
        (sums[:q_w] * norm_factor).reshape(1, q_w),
        (sums[q_w:] * norm_factor).reshape(2, p_w),
    )


def solution(mesh):
    in_specs = (
        P("dp", "ctx", None),
        P("dp", "ctx", None),
        P("dp", "ctx", None),
        P("dp", "ctx", None),
        P("dp", None),
        P("dp", "ctx"),
    )
    out_specs = (
        P("dp", "ctx", None),
        P("dp", "ctx", None),
        P("dp", "ctx", None),
        P("ctx", "dp"),
        P(None, "dp"),
    )
    return jax.shard_map(
        per_device, mesh=mesh, in_specs=in_specs, out_specs=out_specs, check_vma=False
    )
```

time: 307 us -> 65.2 us (0.21)
  blocking collectives: 115 us -> 0 us
  matrix products: 78 us -> 0 us
  local copies, waits for them, and re-layouts: 57.1 us -> 5.42 us
  starting transfers between devices: 25.7 us -> 12.8 us
  Pallas kernels: 0 us -> 12.5 us
  waiting for transfers between devices: 17.7 us -> 27.2 us
    dot_general x96 -> x0, matrix products: 78 us -> none  [the longest x16 26.7 us: head_pass(): jnp.einsum('qk,qd->kd', probs_low, cot_one, preferred_element_type=jnp.fl...]
    all_gather x2 -> x0, blocking collectives: 62.1 us -> none  [carried_in(): everything = jax.tree.map(lambda part: lax.all_gather(part, axis), value)]
    psum x2 -> x0, blocking collectives: 52.9 us -> none  [the longest x1 37 us: from_root(): return lax.psum(kept, axis)]
    ppermute x0 -> x10, waiting for transfers between devices: none -> 22.4 us  [the longest x4 22.3 us: shift(): lax.ppermute(array, 'ctx', [(i, (i + 2 * by) % n_ctx) for i in range(n_ct...]
    all_to_all x7 -> x1, starting transfers between devices: 25.7 us -> 6.07 us  [per_device(): sums = jnp.sum(lax.all_to_all(sends, ('dp', 'ctx'), 0, 0), axis=0)]
    unnamed x27 -> x32, local copies, waits for them, and re-layouts: 22.8 us -> 3.56 us
    dynamic_slice x40 -> x0, local copies, waits for them, and re-layouts: 15.3 us -> none  [the longest x32 15.2 us: attend_heads(): lax.map(head_pass, (to_items(query_here, heads_dev), widen(key_here), wid...]
    all_to_all x7 -> x1, waiting for transfers between devices: 17.7 us -> 4.81 us  [per_device(): sums = jnp.sum(lax.all_to_all(sends, ('dp', 'ctx'), 0, 0), axis=0)]
  transfers between devices with their start and end apart: 7 -> 11, of which waited for: 5 -> 5; matrix products, arithmetic and copies ran while one was open for 12% -> 7% of each run, Pallas kernels for 0% -> 19%
where the time goes in v1:
time: 65.2 us; the launch traced here: 64.7 us
  waiting for transfers between devices  27.2 us (42%)
  starting transfers between devices  12.8 us (20%)
  Pallas kernels  12.5 us (19%)
  other arithmetic  5.91 us (9%)
  local copies, waits for them, and re-layouts  5.42 us (8%)
  between operations  0.89 us (1%)
    ppermute x4, waiting for transfers between devices, shift(): lax.ppermute(array, 'ctx', [(i, (i + 2 * by) % n_ctx) for i in range(n_ct...  22.3 us
    pallas_call x2, Pallas kernels, attend(): pl.pallas_call(functools.partial(attend_kernel, n_pieces, tok, step, doc,...  12.5 us
    all_to_all x1, starting transfers between devices, per_device(): sums = jnp.sum(lax.all_to_all(sends, ('dp', 'ctx'), 0, 0), axis=0)  6.07 us
    ppermute x4, starting transfers between devices, shift(): lax.ppermute(array, 'ctx', [(i, (i + 2 * by) % n_ctx) for i in range(n_ct...  5.3 us
    all_to_all x1, waiting for transfers between devices, per_device(): sums = jnp.sum(lax.all_to_all(sends, ('dp', 'ctx'), 0, 0), axis=0)  4.81 us
    unnamed x32, local copies, waits for them, and re-layouts  3.56 us
    concatenate x1, other arithmetic, per_device(): jnp.concatenate(query_grads, axis=0)  2.2 us
    ppermute x6, starting transfers between devices, to_sibling(): return lax.ppermute(array, 'ctx', [(i, i ^ 1) for i in range(n_ctx)])  1.44 us
  transfers between devices with their start and end apart: 11, of which 5 were waited for; matrix products, arithmetic and copies ran while one was open for 7% of the time, Pallas kernels for 19%

profile of v1, /device:TPU:0, one launch (start us, length us, event | category | flops | bytes accessed | tf_op | source)
XLA Modules:
  0.0 64.7 jit_solution(7701849838896165810)
XLA Ops:
  0.6 1.1 %slice_bitcast_fusion.2 = (bf16[64,1024]{1,0:T(8,128)(2,1)S(1)}, bf16[64,1024]{1,0:T(8,128)(2,1)S(1)}, bf16[64,1024]{1,0:T(8,128)(2,1)S(1)}, bf16[64,1024]{1,0:T(8,128)(2,1)S(1)}) fusion(bf16[2,64,1024]{2,1,0:T(8,128)(2,1)} %param.8, bf16[2,64,1024]{2,1,0:T(8,128)(2,1)} %param.7), kind=kLoop, calls=%fused_computation.15 | loop fusion | bytes 1048576 | tf_op jit(solution)/shard_map/squeeze | solution.py:142
  1.8 0.0 copy-start.1
  1.8 3.1 %collective-permute-start.1 = (bf16[64,2048]{1,0:T(8,128)(2,1)S(1)}, bf16[64,2048]{1,0:T(8,128)(2,1)S(1)}, u32[]{:S(2)}, u32[]{:S(2)}) collective-permute-start(bf16[64,2048]{1,0:T(8,128)(2,1)S(1)} %pad_maximum_fusion.1.refs_5_.refs_6_), channel_id=1, source_target_pairs={{0,2},{1,3},{2,0},{3,1},{4,6},{5,7},{6,4},{7,5},{8,10},{9,11},{10,... | collective-permute-start | bytes 786440 | tf_op jit(solution)/shard_map/ppermute | solution.py:140
  4.9 0.0 copy-start
  4.9 0.1 collective-permute-start.4
  5.0 0.0 copy-done.1
  5.0 0.1 collective-permute-start
  5.1 7.0 %collective-permute-done.1.refs_9_.refs_10_ = bf16[64,2048]{1,0:T(8,128)(2,1)S(1)} collective-permute-done((bf16[64,2048]{1,0:T(8,128)(2,1)S(1)}, bf16[64,2048]{1,0:T(8,128)(2,1)S(1)}, u32[]{:S(2)}, u32[]{:S(2)}) %collective-permute-start.1) | collective-permute-done | bytes 262176 | tf_op jit(solution)/shard_map/ppermute | solution.py:140
  12.0 0.0 copy-start.3
  12.0 0.0 collective-permute-start.2
  12.0 0.5 collective-permute-start.3
  12.5 4.3 %collective-permute-done.4.refs_9_.refs_10_ = bf16[64,2048]{1,0:T(8,128)(2,1)S(1)} collective-permute-done((bf16[64,2048]{1,0:T(8,128)(2,1)S(1)}, bf16[64,2048]{1,0:T(8,128)(2,1)S(1)}, u32[]{:S(2)}, u32[]{:S(2)}) %collective-permute-start.4) | collective-permute-done | bytes 262176 | tf_op jit(solution)/shard_map/ppermute | solution.py:140
  16.8 0.0 copy-start.2
  16.8 0.0 collective-permute-start.5
  16.8 0.0 collective-permute-done.refs_7_.refs_8_
  16.8 0.0 copy-start.6
  16.8 0.0 collective-permute-done.2.refs_11_.refs_12_
  16.8 0.0 copy-start.7
  16.8 0.0 copy-done.3
  16.8 0.7 %copy-done.6 = bf16[64,2048]{1,0:T(8,128)(2,1)} copy-done((bf16[64,2048]{1,0:T(8,128)(2,1)}, bf16[64,2048]{1,0:T(8,128)(2,1)S(1)}, u32[]{:S(2)}) %copy-start.6) | copy-done | bytes 262168
  17.5 0.1 copy-done.7
  17.6 6.2 %attend.2 = (bf16[1,64,4096]{2,1,0:T(8,128)(2,1)}, f32[2,2,64,1024]{3,2,1,0:T(8,128)}, bf16[2,2,64,1024]{3,2,1,0:T(8,128)(2,1)}, f32[1,4096]{1,0:T(1,128)}, f32[1,1024]{1,0:T(1,128)}, /*index=5*/f32[1,1024]{1,0:T(1,128)}) custom-call(s32[1]{0:T(128)} %bitcast.refs_0_, s32[2,128]{1,0:T(2,128)} %refs_1_.3, s32[2,64]{1,0:T(2,128)} %refs_2_.3, ...), custom_call_target="tpu_custom_call" | custom-call | tf_op jit(solution)/shard_map/attend/pallas_call | solution.py:97
  23.8 0.0 copy-done
  23.8 0.0 copy-done.2
  23.8 0.0 copy-start.11
  23.9 0.5 collective-permute-start.6
  24.4 0.0 collective-permute-done.3.refs_7_.refs_8_
  24.4 0.0 copy-start.4
  24.4 0.0 collective-permute-done.5.refs_11_.refs_12_
  24.4 0.7 %copy-done.4 = bf16[64,2048]{1,0:T(8,128)(2,1)} copy-done((bf16[64,2048]{1,0:T(8,128)(2,1)}, bf16[64,2048]{1,0:T(8,128)(2,1)S(1)}, u32[]{:S(2)}) %copy-start.4) | copy-done | bytes 262168
  25.1 0.0 copy-start.5
  25.1 0.7 %copy-done.5 = bf16[64,2048]{1,0:T(8,128)(2,1)} copy-done((bf16[64,2048]{1,0:T(8,128)(2,1)}, bf16[64,2048]{1,0:T(8,128)(2,1)S(1)}, u32[]{:S(2)}) %copy-start.5) | copy-done | bytes 262168
  25.8 6.3 %attend.3 = (bf16[1,64,4096]{2,1,0:T(8,128)(2,1)}, f32[2,2,64,1024]{3,2,1,0:T(8,128)}, bf16[2,2,64,1024]{3,2,1,0:T(8,128)(2,1)}, f32[1,4096]{1,0:T(1,128)}, f32[1,1024]{1,0:T(1,128)}, /*index=5*/f32[1,1024]{1,0:T(1,128)}) custom-call(s32[1]{0:T(128)} %bitcast.refs_0_, s32[2,128]{1,0:T(2,128)} %refs_1_.3, s32[2,64]{1,0:T(2,128)} %refs_2_.3, ...), custom_call_target="tpu_custom_call" | custom-call | tf_op jit(solution)/shard_map/attend/pallas_call | solution.py:97
  32.1 0.0 copy-done.11
  32.2 0.7 %add.43 = f32[1,4096]{1,0:T(1,128)S(1)} add(f32[1,4096]{1,0:T(1,128)S(1)} %copy-done.11, f32[1,4096]{1,0:T(1,128)} %get-tuple-element.24) | non-fusion elementwise | flops 4096 | bytes 49152 | tf_op jit(solution)/shard_map/add | solution.py:155
  32.9 0.0 copy-start.13
  32.9 0.0 copy-start.15
  32.9 0.6 copy-done.13
  33.6 0.0 copy-done.15
  33.6 0.7 %copy-done.12 = f32[1,1024]{1,0:T(1,128)S(1)} copy-done((f32[1,1024]{1,0:T(1,128)S(1)}, f32[1,1024]{1,0:T(1,128)}, u32[]{:S(2)}) %copy-start.12) | copy-done | bytes 4120
  34.3 0.0 copy-done.14
  34.3 0.7 %all_to_all.6 = f32[32,1,384]{2,1,0:T(1,128)} reshape(f32[8,4,384]{2,1,0:T(4,128)S(1)} %pad_maximum_fusion.5) | data formatting | bytes 98304 | tf_op jit(solution)/shard_map/all_to_all | solution.py:174
  35.0 6.1 %all-to-all-start = ((f32[32,1,384]{2,1,0:T(1,128)}), f32[32,1,384]{2,1,0:T(1,128)S(1)}, u32[]{:S(2)}, u32[]{:S(2)}) async-start(f32[32,1,384]{2,1,0:T(1,128)} %all_to_all.6), calls=%async_computation | async-start | bytes 98304 | tf_op jit(solution)/shard_map/all_to_all | solution.py:174
  41.1 0.3 collective-permute-start.8
  41.4 0.0 copy-done.10
  41.4 2.2 %pad_maximum_fusion = bf16[2,64,4096]{2,1,0:T(8,128)(2,1)} fusion(bf16[1,64,4096]{2,1,0:T(8,128)(2,1)} %get-tuple-element.18, bf16[1,64,4096]{2,1,0:T(8,128)(2,1)S(1)} %copy-done.10), kind=kLoop, calls=%fused_computation | loop fusion | flops 524288 | bytes 2097152 | tf_op jit(solution)/shard_map/concatenate | solution.py:177
  43.6 4.8 %all-to-all-done = f32[32,1,384]{2,1,0:T(1,128)S(1)} async-done(((f32[32,1,384]{2,1,0:T(1,128)}), f32[32,1,384]{2,1,0:T(1,128)S(1)}, u32[]{:S(2)}, u32[]{:S(2)}) %all-to-all-start) | async-done | bytes 49184 | tf_op jit(solution)/shard_map/all_to_all | solution.py:174
  48.4 0.1 reduce_sum.9
  48.5 0.6 multiply_bitcast_fusion
  49.0 0.0 collective-permute-done.6
  49.0 0.0 copy-done.8
  49.1 0.1 fusion.2
  49.1 0.5 collective-permute-start.7
  49.6 0.5 multiply_bitcast_fusion.1
  50.2 0.0 collective-permute-done.8
  50.2 0.0 copy-done.9
  50.2 0.1 fusion.3
  50.2 1.6 %collective-permute-start.9 = (bf16[2,64,1024]{2,1,0:T(8,128)(2,1)S(1)}, bf16[2,64,1024]{2,1,0:T(8,128)(2,1)S(1)}, u32[]{:S(2)}, u32[]{:S(2)}) collective-permute-start(bf16[2,64,1024]{2,1,0:T(8,128)(2,1)S(1)} %fusion.3), channel_id=1, source_target_pairs={{0,2},{1,3},{2,0},{3,1},{4,6},{5,7},{6,4},{7,5},{8,10},{9,11},{10,... | collective-permute-start | bytes 786440 | tf_op jit(solution)/shard_map/ppermute | solution.py:140
  51.9 6.5 %collective-permute-done.7 = bf16[2,64,1024]{2,1,0:T(8,128)(2,1)S(1)} collective-permute-done((bf16[2,64,1024]{2,1,0:T(8,128)(2,1)S(1)}, bf16[2,64,1024]{2,1,0:T(8,128)(2,1)S(1)}, u32[]{:S(2)}, u32[]{:S(2)}) %collective-permute-start.7) | collective-permute-done | bytes 262176 | tf_op jit(solution)/shard_map/ppermute | solution.py:140
  58.4 0.1 fusion.1
  58.5 4.6 %collective-permute-done.9 = bf16[2,64,1024]{2,1,0:T(8,128)(2,1)S(1)} collective-permute-done((bf16[2,64,1024]{2,1,0:T(8,128)(2,1)S(1)}, bf16[2,64,1024]{2,1,0:T(8,128)(2,1)S(1)}, u32[]{:S(2)}, u32[]{:S(2)}) %collective-permute-start.9) | collective-permute-done | bytes 262176 | tf_op jit(solution)/shard_map/ppermute | solution.py:140
  63.1 0.1 fusion
  63.3 0.7 %pad_maximum_fusion.4 = bf16[2,64,1024]{2,1,0:T(8,128)(2,1)} fusion(bf16[1,64,1024]{2,1,0:T(8,128)(2,1)S(1)} %get-tuple-element.31, bf16[1,64,1024]{2,1,0:T(8,128)(2,1)S(1)} %get-tuple-element.29), kind=kLoop, calls=%fused_computation.12 | loop fusion | flops 131072 | bytes 524288 | tf_op jit(solution)/shard_map/stack | solution.py:166
  64.0 0.7 %pad_maximum_fusion.3 = bf16[2,64,1024]{2,1,0:T(8,128)(2,1)} fusion(bf16[1,64,1024]{2,1,0:T(8,128)(2,1)S(1)} %get-tuple-element.32, bf16[1,64,1024]{2,1,0:T(8,128)(2,1)S(1)} %get-tuple-element.30), kind=kLoop, calls=%fused_computation.11 | loop fusion | flops 131072 | bytes 524288 | tf_op jit(solution)/shard_map/stack | solution.py:165
  (15 shorter events, 0.1 us)
Async XLA Ops:
  1.8 3.2 %copy-start.1 = (bf16[64,2048]{1,0:T(8,128)(2,1)}, bf16[64,2048]{1,0:T(8,128)(2,1)S(1)}, u32[]{:S(2)}) copy-start(bf16[64,2048]{1,0:T(8,128)(2,1)S(1)} %pad_maximum_fusion.1.refs_5_.refs_6_) | copy-start | bytes 786436
  1.8 10.2 %collective-permute-start.1 = (bf16[64,2048]{1,0:T(8,128)(2,1)S(1)}, bf16[64,2048]{1,0:T(8,128)(2,1)S(1)}, u32[]{:S(2)}, u32[]{:S(2)}) collective-permute-start(bf16[64,2048]{1,0:T(8,128)(2,1)S(1)} %pad_maximum_fusion.1.refs_5_.refs_6_), channel_id=1, source_target_pairs={{0,2},{1,3},{2,0},{3,1},{4,6},{5,7},{6,4},{7,5},{8,10},{9,11},{10,... | collective-permute-start | bytes 786440 | tf_op jit(solution)/shard_map/ppermute | solution.py:140
  4.9 18.9 %copy-start = (bf16[64,2048]{1,0:T(8,128)(2,1)}, bf16[64,2048]{1,0:T(8,128)(2,1)S(1)}, u32[]{:S(2)}) copy-start(bf16[64,2048]{1,0:T(8,128)(2,1)S(1)} %pad_maximum_fusion.2.refs_5_.refs_6_) | copy-start | bytes 786436
  4.9 11.9 %collective-permute-start.4 = (bf16[64,2048]{1,0:T(8,128)(2,1)S(1)}, bf16[64,2048]{1,0:T(8,128)(2,1)S(1)}, u32[]{:S(2)}, u32[]{:S(2)}) collective-permute-start(bf16[64,2048]{1,0:T(8,128)(2,1)S(1)} %pad_maximum_fusion.2.refs_5_.refs_6_), channel_id=1, source_target_pairs={{0,2},{1,3},{2,0},{3,1},{4,6},{5,7},{6,4},{7,5},{8,10},{9,11},{10,... | collective-permute-start | bytes 786440 | tf_op jit(solution)/shard_map/ppermute | solution.py:140
  5.0 11.8 %collective-permute-start = (bf16[64,2048]{1,0:T(8,128)(2,1)S(1)}, bf16[64,2048]{1,0:T(8,128)(2,1)S(1)}, u32[]{:S(2)}, u32[]{:S(2)}) collective-permute-start(bf16[64,2048]{1,0:T(8,128)(2,1)S(1)} %pad_maximum_fusion.1.refs_5_.refs_6_), channel_id=1, source_target_pairs={{0,1},{1,0},{2,3},{3,2},{4,5},{5,4},{6,7},{7,6},{8,9},{9,8},{10,11... | collective-permute-start | bytes 786440 | tf_op jit(solution)/shard_map/ppermute | solution.py:137
  12.0 4.8 %copy-start.3 = (bf16[64,2048]{1,0:T(8,128)(2,1)}, bf16[64,2048]{1,0:T(8,128)(2,1)S(1)}, u32[]{:S(2)}) copy-start(bf16[64,2048]{1,0:T(8,128)(2,1)S(1)} %collective-permute-done.1.refs_9_.refs_10_) | copy-start | bytes 786436
  12.0 4.8 %collective-permute-start.2 = (bf16[64,2048]{1,0:T(8,128)(2,1)S(1)}, bf16[64,2048]{1,0:T(8,128)(2,1)S(1)}, u32[]{:S(2)}, u32[]{:S(2)}) collective-permute-start(bf16[64,2048]{1,0:T(8,128)(2,1)S(1)} %collective-permute-done.1.refs_9_.refs_10_), channel_id=1, source_target_pairs={{0,1},{1,0},{2,3},{3,2},{4,5},{5,4},{6,7},{7,6},{8,9},{9,8},{10,11... | collective-permute-start | bytes 786440 | tf_op jit(solution)/shard_map/ppermute | solution.py:137
  12.0 12.4 %collective-permute-start.3 = (bf16[64,2048]{1,0:T(8,128)(2,1)S(1)}, bf16[64,2048]{1,0:T(8,128)(2,1)S(1)}, u32[]{:S(2)}, u32[]{:S(2)}) collective-permute-start(bf16[64,2048]{1,0:T(8,128)(2,1)S(1)} %pad_maximum_fusion.2.refs_5_.refs_6_), channel_id=1, source_target_pairs={{0,1},{1,0},{2,3},{3,2},{4,5},{5,4},{6,7},{7,6},{8,9},{9,8},{10,11... | collective-permute-start | bytes 786440 | tf_op jit(solution)/shard_map/ppermute | solution.py:137
  16.8 7.1 %copy-start.2 = (bf16[64,2048]{1,0:T(8,128)(2,1)}, bf16[64,2048]{1,0:T(8,128)(2,1)S(1)}, u32[]{:S(2)}) copy-start(bf16[64,2048]{1,0:T(8,128)(2,1)S(1)} %collective-permute-done.4.refs_9_.refs_10_) | copy-start | bytes 786436
  16.8 7.6 %collective-permute-start.5 = (bf16[64,2048]{1,0:T(8,128)(2,1)S(1)}, bf16[64,2048]{1,0:T(8,128)(2,1)S(1)}, u32[]{:S(2)}, u32[]{:S(2)}) collective-permute-start(bf16[64,2048]{1,0:T(8,128)(2,1)S(1)} %collective-permute-done.4.refs_9_.refs_10_), channel_id=1, source_target_pairs={{0,1},{1,0},{2,3},{3,2},{4,5},{5,4},{6,7},{7,6},{8,9},{9,8},{10,11... | collective-permute-start | bytes 786440 | tf_op jit(solution)/shard_map/ppermute | solution.py:137
  16.8 0.7 %copy-start.6 = (bf16[64,2048]{1,0:T(8,128)(2,1)}, bf16[64,2048]{1,0:T(8,128)(2,1)S(1)}, u32[]{:S(2)}) copy-start(bf16[64,2048]{1,0:T(8,128)(2,1)S(1)} %collective-permute-done.refs_7_.refs_8_) | copy-start | bytes 786436
  16.8 0.8 %copy-start.7 = (bf16[64,2048]{1,0:T(8,128)(2,1)}, bf16[64,2048]{1,0:T(8,128)(2,1)S(1)}, u32[]{:S(2)}) copy-start(bf16[64,2048]{1,0:T(8,128)(2,1)S(1)} %collective-permute-done.2.refs_11_.refs_12_) | copy-start | bytes 786436
  23.8 8.3 %copy-start.11 = (f32[1,4096]{1,0:T(1,128)S(1)}, f32[1,4096]{1,0:T(1,128)}, u32[]{:S(2)}) copy-start(f32[1,4096]{1,0:T(1,128)} %get-tuple-element.23) | copy-start | bytes 49156
  23.9 25.2 %collective-permute-start.6 = (bf16[2,2,64,1024]{3,2,1,0:T(8,128)(2,1)}, bf16[2,2,64,1024]{3,2,1,0:T(8,128)(2,1)S(1)}, u32[]{:S(2)}, u32[]{:S(2)}) collective-permute-start(bf16[2,2,64,1024]{3,2,1,0:T(8,128)(2,1)} %get-tuple-element.20), channel_id=1, source_target_pairs={{0,1},{1,0},{2,3},{3,2},{4,5},{5,4},{6,7},{7,6},{8,9},{9,8},{10,11... | collective-permute-start | bytes 1572872 | tf_op jit(solution)/shard_map/ppermute | solution.py:137
  24.4 0.7 %copy-start.4 = (bf16[64,2048]{1,0:T(8,128)(2,1)}, bf16[64,2048]{1,0:T(8,128)(2,1)S(1)}, u32[]{:S(2)}) copy-start(bf16[64,2048]{1,0:T(8,128)(2,1)S(1)} %collective-permute-done.3.refs_7_.refs_8_) | copy-start | bytes 786436
  25.1 0.7 %copy-start.5 = (bf16[64,2048]{1,0:T(8,128)(2,1)}, bf16[64,2048]{1,0:T(8,128)(2,1)S(1)}, u32[]{:S(2)}) copy-start(bf16[64,2048]{1,0:T(8,128)(2,1)S(1)} %collective-permute-done.5.refs_11_.refs_12_) | copy-start | bytes 786436
  25.8 15.6 %copy-start.10 = (bf16[1,64,4096]{2,1,0:T(8,128)(2,1)S(1)}, bf16[1,64,4096]{2,1,0:T(8,128)(2,1)}, u32[]{:S(2)}) copy-start(bf16[1,64,4096]{2,1,0:T(8,128)(2,1)} %get-tuple-element.17) | copy-start | bytes 1572868
  32.9 0.7 %copy-start.13 = (f32[1,1024]{1,0:T(1,128)S(1)}, f32[1,1024]{1,0:T(1,128)}, u32[]{:S(2)}) copy-start(f32[1,1024]{1,0:T(1,128)} %get-tuple-element.27) | copy-start | bytes 12292
  32.9 0.7 %copy-start.15 = (f32[1,1024]{1,0:T(1,128)S(1)}, f32[1,1024]{1,0:T(1,128)}, u32[]{:S(2)}) copy-start(f32[1,1024]{1,0:T(1,128)} %get-tuple-element.28) | copy-start | bytes 12292
  33.6 0.7 %copy-start.12 = (f32[1,1024]{1,0:T(1,128)S(1)}, f32[1,1024]{1,0:T(1,128)}, u32[]{:S(2)}) copy-start(f32[1,1024]{1,0:T(1,128)} %get-tuple-element.25) | copy-start | bytes 12292
  33.6 0.7 %copy-start.14 = (f32[1,1024]{1,0:T(1,128)S(1)}, f32[1,1024]{1,0:T(1,128)}, u32[]{:S(2)}) copy-start(f32[1,1024]{1,0:T(1,128)} %get-tuple-element.26) | copy-start | bytes 12292
  35.0 13.4 %all-to-all-start = ((f32[32,1,384]{2,1,0:T(1,128)}), f32[32,1,384]{2,1,0:T(1,128)S(1)}, u32[]{:S(2)}, u32[]{:S(2)}) async-start(f32[32,1,384]{2,1,0:T(1,128)} %all_to_all.6), calls=%async_computation | async-start | bytes 98304 | tf_op jit(solution)/shard_map/all_to_all | solution.py:174
  41.1 9.1 %collective-permute-start.8 = (bf16[2,2,64,1024]{3,2,1,0:T(8,128)(2,1)}, bf16[2,2,64,1024]{3,2,1,0:T(8,128)(2,1)S(1)}, u32[]{:S(2)}, u32[]{:S(2)}) collective-permute-start(bf16[2,2,64,1024]{3,2,1,0:T(8,128)(2,1)} %get-tuple-element.22), channel_id=1, source_target_pairs={{0,1},{1,0},{2,3},{3,2},{4,5},{5,4},{6,7},{7,6},{8,9},{9,8},{10,11... | collective-permute-start | bytes 1572872 | tf_op jit(solution)/shard_map/ppermute | solution.py:137
  41.4 7.7 %copy-start.8 = (f32[2,2,64,1024]{3,2,1,0:T(8,128)S(1)}, f32[2,2,64,1024]{3,2,1,0:T(8,128)}, u32[]{:S(2)}) copy-start(f32[2,2,64,1024]{3,2,1,0:T(8,128)} %get-tuple-element.19) | copy-start | bytes 3145732
  43.6 6.6 %copy-start.9 = (f32[2,2,64,1024]{3,2,1,0:T(8,128)S(1)}, f32[2,2,64,1024]{3,2,1,0:T(8,128)}, u32[]{:S(2)}) copy-start(f32[2,2,64,1024]{3,2,1,0:T(8,128)} %get-tuple-element.21) | copy-start | bytes 3145732
  49.1 9.2 %collective-permute-start.7 = (bf16[2,64,1024]{2,1,0:T(8,128)(2,1)S(1)}, bf16[2,64,1024]{2,1,0:T(8,128)(2,1)S(1)}, u32[]{:S(2)}, u32[]{:S(2)}) collective-permute-start(bf16[2,64,1024]{2,1,0:T(8,128)(2,1)S(1)} %fusion.2), channel_id=1, source_target_pairs={{0,2},{1,3},{2,0},{3,1},{4,6},{5,7},{6,4},{7,5},{8,10},{9,11},{10,... | collective-permute-start | bytes 786440 | tf_op jit(solution)/shard_map/ppermute | solution.py:140
  50.2 12.9 %collective-permute-start.9 = (bf16[2,64,1024]{2,1,0:T(8,128)(2,1)S(1)}, bf16[2,64,1024]{2,1,0:T(8,128)(2,1)S(1)}, u32[]{:S(2)}, u32[]{:S(2)}) collective-permute-start(bf16[2,64,1024]{2,1,0:T(8,128)(2,1)S(1)} %fusion.3), channel_id=1, source_target_pairs={{0,2},{1,3},{2,0},{3,1},{4,6},{5,7},{6,4},{7,5},{8,10},{9,11},{10,... | collective-permute-start | bytes 786440 | tf_op jit(solution)/shard_map/ppermute | solution.py:140

commit v2 on v1

v2 whole, which is shorter than its diff:
```python
import functools
import math

import jax
import jax.numpy as jnp
from jax import lax
from jax.experimental import pallas as pl
from jax.experimental.pallas import tpu as pltpu
from jax.sharding import PartitionSpec as P


H = 32
KVH = 8
HD = 128
NB = 16
GROUP = H // KVH
CORES = 2
HEADS = KVH // CORES
QW = HEADS * GROUP * HD
KW = HEADS * HD

NT = (((1,), (1,)), ((), ()))
NN = (((1,), (0,)), ((), ()))
TN = (((0,), (0,)), ((), ()))
BF = jnp.bfloat16
F32 = jnp.float32


def dot(a, b, dims):
    return lax.dot_general(a, b, dims, preferred_element_type=F32)


def whole(shape):
    return pl.BlockSpec(shape, lambda *_: (0,) * len(shape))


HELD_CTX = 4


def fits(n_ctx):
    return n_ctx <= HELD_CTX


def vmem(shape, dtype):
    if fits(lax.axis_size("ctx")):
        return pltpu.VMEM(shape, dtype)
    return jax.ShapeDtypeStruct(shape, dtype)


def held(array):
    if fits(lax.axis_size("ctx")):
        return pltpu.with_memory_space_constraint(array, pltpu.VMEM)
    return array


def grant(mib):
    if fits(lax.axis_size("ctx")):
        return pltpu.CompilerParams(vmem_limit_bytes=mib << 20)
    return None


IN_VMEM = pl.BlockSpec(memory_space=pltpu.VMEM)
IN_SMEM = pl.BlockSpec(memory_space=pltpu.SMEM)


def split_kv_kernel(place_ref, key_mine, value_mine, key_other, value_other, *outs):
    docs = key_mine.shape[0]
    for d in range(docs):
        outs[2 * d][0] = key_mine[d]
        outs[2 * d][1] = value_mine[d]
        outs[2 * d + 1][0] = key_other[d]
        outs[2 * d + 1][1] = value_other[d]


def split_kv(place, key_in, value_in):
    docs, tok = key_in.shape[:2]
    mine = pl.BlockSpec((docs, tok, KW), lambda g, p: (0, 0, p[0] % CORES))
    other = pl.BlockSpec((docs, tok, KW), lambda g, p: (0, 0, 1 - p[0] % CORES))
    shape = (2, tok, KW)
    outs = pl.pallas_call(
        split_kv_kernel,
        grid_spec=pltpu.PrefetchScalarGridSpec(
            num_scalar_prefetch=1,
            grid=(1,),
            in_specs=[mine, mine, other, other],
            out_specs=[IN_VMEM] * (2 * docs),
        ),
        out_shape=[vmem(shape, BF)] * (2 * docs),
        compiler_params=grant(4),
        name="split_kv",
    )(place, key_in, value_in, key_in, value_in)
    return outs[0::2], outs[1::2]


def weigh_kernel(
    place_ref, masked_ref, bucket_ref, query_own, grad_own, query_ref, grad_ref, *outs
):
    docs, tok = query_ref.shape[:2]
    rows = lax.broadcasted_iota(jnp.int32, (tok, masked_ref.shape[1]), 0) + place_ref[0] * tok
    lane = lax.broadcasted_iota(jnp.int32, (tok, tok), 1)
    line = lax.broadcasted_iota(jnp.int32, (tok, tok), 0)
    for d in range(docs):
        hit = jnp.where(masked_ref[d : d + 1, :] == rows, 1.0, 0.0)
        is_masked = jnp.max(hit, axis=1, keepdims=True)
        spread = jnp.where(lane == line, bucket_ref[d : d + 1, :].astype(F32), 0.0)
        level = jnp.sum(spread, axis=1, keepdims=True)
        weight = is_masked * NB / (level + 1.0)
        outs[2 * d][0] = query_own[d]
        outs[2 * d][1] = (grad_own[d].astype(F32) * weight).astype(BF)
        outs[2 * d + 1][0] = query_ref[d]
        outs[2 * d + 1][1] = (grad_ref[d].astype(F32) * weight).astype(BF)


def weigh(place, masked, bucket, query, out_grad):
    docs, tok = query.shape[:2]
    own = pl.BlockSpec((docs, tok, QW), lambda g, p: (0, 0, p[0] % CORES))
    other = pl.BlockSpec((docs, tok, QW), lambda g, p: (0, 0, 1 - p[0] % CORES))
    outs = pl.pallas_call(
        weigh_kernel,
        grid_spec=pltpu.PrefetchScalarGridSpec(
            num_scalar_prefetch=1,
            grid=(1,),
            in_specs=[whole(masked.shape), whole(bucket.shape), own, own, other, other],
            out_specs=[IN_VMEM] * (2 * docs),
        ),
        out_shape=[vmem((2, tok, QW), BF)] * (2 * docs),
        compiler_params=grant(8),
        name="weigh",
    )(place, masked, bucket, query, out_grad, query, out_grad)
    return outs[0::2], outs[1::2]


def attend_kernel(n_pieces, tok, has_before, own_ref, swap_ref, *refs):
    piece_refs = refs[:n_pieces]
    before_refs = refs[n_pieces : n_pieces + 2 * has_before]
    dq_ref, dq_sib_ref, qsum_ref, kvsum_ref, near_ref, *far_refs = refs[
        n_pieces + 2 * has_before :
    ]
    inv_root = 1.0 / math.sqrt(HD)
    for g in range(HEADS):
        cols = [slice((g * GROUP + h) * HD, (g * GROUP + h + 1) * HD) for h in range(GROUP)]
        kv = slice(g * HD, (g + 1) * HD)
        q_rows, c_rows = (
            jnp.concatenate([ref[which, :, c] for ref in (own_ref, swap_ref) for c in cols], axis=0)
            for which in (0, 1)
        )
        keys, values = (
            jnp.concatenate([r[which, :, kv] for r in piece_refs], axis=0) for which in (0, 1)
        )
        scores = dot(keys, q_rows, NT)
        prob_grad = dot(values, c_rows, NT)
        top = jnp.max(scores, axis=0, keepdims=True)
        expo = jnp.exp((scores - top) * inv_root)
        probs = expo * (1.0 / jnp.sum(expo, axis=0, keepdims=True))
        low = probs.astype(BF)
        delta = jnp.sum(low.astype(F32) * prob_grad, axis=0, keepdims=True)
        score_low = (probs * (prob_grad - delta) * inv_root).astype(BF)
        dv = dot(low, c_rows, NN)
        dk = dot(score_low, q_rows, NN)
        dq = dot(score_low, keys, TN)
        for h, c in enumerate(cols):
            part = dq[h * tok : (h + 1) * tok]
            other = dq[(GROUP + h) * tok : (GROUP + h + 1) * tok]
            dq_ref[:, c] = part.astype(BF)
            dq_sib_ref[:, c] = other.astype(BF)
            row = g * GROUP + h
            total = jnp.sum(part + other, axis=0, keepdims=True)
            if has_before:
                total = total + before_refs[0][row : row + 1]
            qsum_ref[row : row + 1] = total
        for which, full in ((0, dk), (1, dv)):
            side = slice(which * HD, (which + 1) * HD)
            total = jnp.sum(full, axis=0, keepdims=True)
            if has_before:
                total = total + before_refs[1][g : g + 1, side]
            kvsum_ref[g : g + 1, side] = total
            near_ref[which, :, kv] = full[:tok]
            for piece in range(1, n_pieces):
                part = full[piece * tok : (piece + 1) * tok]
                far_refs[piece - 1][which, :, kv] = part.astype(BF)


def attend(own, swap, pieces, before):
    tok = own.shape[1]
    n_pieces = len(pieces)
    args = [own, swap, *pieces, *before]
    outs = pl.pallas_call(
        functools.partial(attend_kernel, n_pieces, tok, bool(before)),
        in_specs=[IN_VMEM] * len(args),
        out_specs=[IN_VMEM] * (5 + n_pieces - 1),
        out_shape=[
            vmem((tok, QW), BF),
            vmem((tok, QW), BF),
            vmem((HEADS * GROUP, HD), F32),
            vmem((HEADS, 2 * HD), F32),
            vmem((2, tok, KW), F32),
            *[vmem((2, tok, KW), BF)] * (n_pieces - 1),
        ],
        compiler_params=grant(20),
        name="attend",
    )(*[held(arg) for arg in args])
    return outs[:2], outs[2:4], outs[4], outs[5:]


def share_kernel(n_ctx, n_dp, place_ref, qsum_ref, kvsum_ref, out_ref):
    for core in range(CORES):

        @pl.when(place_ref[0] % CORES == core)
        def _():
            out_ref[...] = jnp.zeros(out_ref.shape, F32)
            base = core * H // CORES
            for row in range(HEADS * GROUP):
                out_ref[base + row, :, :HD] = qsum_ref[row : row + 1]
            for c in range(n_ctx):
                for g in range(HEADS):
                    out_ref[c * n_dp + core * HEADS + g, :, HD:] = kvsum_ref[g : g + 1]


def shares_of(place, sums, n_ctx, n_dp):
    qsum, kvsum = sums
    q_w = H * HD // (n_ctx * n_dp)
    p_w = KVH * HD // n_dp
    rows = n_ctx * n_dp
    if q_w == HD and p_w == HD:
        return pl.pallas_call(
            functools.partial(share_kernel, n_ctx, n_dp),
            in_specs=[IN_SMEM, IN_VMEM, IN_VMEM],
            out_specs=IN_VMEM,
            out_shape=vmem((rows, 1, q_w + 2 * p_w), F32),
            compiler_params=grant(2),
            name="share",
        )(place, held(qsum), held(kvsum))
    core = place[0] % CORES

    def both_halves(part):
        return jnp.concatenate([jnp.where(core == c, part, 0.0) for c in range(CORES)], axis=0)

    q_part = both_halves(qsum).reshape(n_ctx, n_dp, q_w)
    pair = both_halves(kvsum)
    pair = jnp.concatenate(
        [pair[:, :HD].reshape(n_dp, p_w), pair[:, HD:].reshape(n_dp, p_w)], axis=1
    )
    pair = jnp.broadcast_to(pair[None], (n_ctx, n_dp, 2 * p_w))
    return jnp.concatenate([q_part, pair], axis=-1).reshape(rows, 1, q_w + 2 * p_w)


def join_q_kernel(docs, place_ref, *refs):
    out_ref = refs[2 * docs]
    for core in range(CORES):

        @pl.when(place_ref[0] % CORES == core)
        def _():
            mine, other = (slice(c * QW, (c + 1) * QW) for c in (core, 1 - core))
            for d in range(docs):
                out_ref[d, :, mine] = refs[2 * d][...]
                out_ref[d, :, other] = refs[2 * d + 1][...]


def join_q(place, parts):
    docs, tok = len(parts), parts[0][0].shape[0]
    shape = (docs, tok, CORES * QW)
    return pl.pallas_call(
        functools.partial(join_q_kernel, docs),
        in_specs=[IN_SMEM] + [IN_VMEM] * (2 * docs),
        out_shape=jax.ShapeDtypeStruct(shape, BF),
        compiler_params=grant(6),
        name="join_q",
    )(place, *[held(part) for pair in parts for part in pair])


def join_kv_kernel(docs, terms, place_ref, *refs):
    key_ref, value_ref = refs[2 * docs * terms :]
    for core in range(CORES):

        @pl.when(place_ref[0] % CORES == core)
        def _():
            for d in range(docs):
                for side, half in ((0, core), (1, 1 - core)):
                    first = (2 * d + side) * terms
                    total = refs[first][...].astype(F32)
                    for ref in refs[first + 1 : first + terms]:
                        total = total + ref[...].astype(F32)
                    cols = slice(half * KW, (half + 1) * KW)
                    key_ref[d, :, cols] = total[0].astype(BF)
                    value_ref[d, :, cols] = total[1].astype(BF)


def join_kv(place, parts):
    docs, terms, tok = len(parts), len(parts[0][0]), parts[0][0][0].shape[1]
    shape = jax.ShapeDtypeStruct((docs, tok, CORES * KW), BF)
    flat = [held(part) for sides in parts for side in sides for part in side]
    return pl.pallas_call(
        functools.partial(join_kv_kernel, docs, terms),
        in_specs=[IN_SMEM] + [IN_VMEM] * len(flat),
        out_shape=[shape, shape],
        compiler_params=grant(6),
        name="join_kv",
    )(place, *flat)


def bias_kernel(norm_factor, q_w, p_w, gathered_ref, query_ref, pair_ref):
    totals = jnp.sum(gathered_ref[...], axis=0) * norm_factor
    query_ref[...] = totals[:, :q_w]
    pair_ref[0:1] = totals[:, q_w : q_w + p_w]
    pair_ref[1:2] = totals[:, q_w + p_w :]


def bias_out(gathered, norm_factor, q_w, p_w):
    return pl.pallas_call(
        functools.partial(bias_kernel, norm_factor, q_w, p_w),
        in_specs=[IN_VMEM],
        out_shape=[
            jax.ShapeDtypeStruct((1, q_w), F32),
            jax.ShapeDtypeStruct((2, p_w), F32),
        ],
        compiler_params=grant(2),
        name="bias_out",
    )(held(gathered))


def hops_of(n_ctx):
    return [(s, x) for s in range(n_ctx // CORES) for x in range(CORES) if s or x]


def step_device(query, key_in, value_in, out_grad, masked, bucket):
    n_ctx = lax.axis_size("ctx")
    n_dp = lax.axis_size("dp")
    docs, tok = query.shape[:2]
    chips = n_ctx // CORES
    hops = hops_of(n_ctx)
    place = lax.axis_index("ctx").astype(jnp.int32).reshape(1)

    def move(array, chip, cross):
        pairs = [(i, (i + CORES * chip) % n_ctx ^ cross) for i in range(n_ctx)]
        return lax.ppermute(array, "ctx", pairs)

    mine, other = split_kv(place, key_in, value_in)
    pieces = [
        [mine[d]] + [move((mine, other)[x][d], s, x) for s, x in hops]
        for d in range(docs)
    ]
    own, sends = weigh(place, masked, bucket, query, out_grad)
    swaps = [move(send, 0, 1) for send in sends]
    q_parts, kv_parts, sums = [], [], ()
    for d in range(docs):
        (dq, dq_sib), sums, near, far = attend(own[d], swaps[d], pieces[d], sums)
        back = {(s, x): move(part, -s, x) for (s, x), part in zip(hops, far)}
        kv_parts.append(
            [
                [near] + [back[s, 0] for s in range(1, chips)],
                [back[s, 1] for s in range(chips)],
            ]
        )
        q_parts.append((dq, move(dq_sib, 0, 1)))

    shares = shares_of(place, sums, n_ctx, n_dp)
    gathered = lax.all_to_all(shares, ("ctx", "dp"), 0, 0)
    norm_factor = 1.0 / math.sqrt(docs * n_dp * tok * n_ctx)
    q_w = H * HD // (n_ctx * n_dp)
    p_w = KVH * HD // n_dp
    key_grad, value_grad = join_kv(place, kv_parts)
    query_grad = join_q(place, q_parts)
    bias_q, bias_kv = bias_out(gathered, norm_factor, q_w, p_w)
    return query_grad, key_grad, value_grad, bias_q, bias_kv


def solution(mesh):
    in_specs = (
        P("dp", "ctx", None),
        P("dp", "ctx", None),
        P("dp", "ctx", None),
        P("dp", "ctx", None),
        P("dp", None),
        P("dp", "ctx"),
    )
    out_specs = (
        P("dp", "ctx", None),
        P("dp", "ctx", None),
        P("dp", "ctx", None),
        P("ctx", "dp"),
        P(None, "dp"),
    )
    return jax.shard_map(
        step_device, mesh=mesh, in_specs=in_specs, out_specs=out_specs, check_vma=False
    )
```

time: 65.2 us -> 47.5 us (0.73)
  waiting for transfers between devices: 27.2 us -> 9.77 us
  blocking collectives: 0 us -> 11.9 us
  other arithmetic: 5.91 us -> 0 us
  Pallas kernels: 12.5 us -> 7.94 us
  local copies, waits for them, and re-layouts: 5.42 us -> 3.21 us
  starting transfers between devices: 12.8 us -> 13.7 us
    ppermute x10 -> x16, waiting for transfers between devices: 22.4 us -> 9.77 us  [move(): return lax.ppermute(array, 'ctx', pairs)]
    all_to_all x0 -> x1, blocking collectives: none -> 11.9 us  [step_device(): gathered = lax.all_to_all(shares, ('ctx', 'dp'), 0, 0)]
    ppermute x10 -> x16, starting transfers between devices: 6.74 us -> 13.7 us  [move(): return lax.ppermute(array, 'ctx', pairs)]
    all_to_all x1 -> x0, starting transfers between devices: 6.07 us -> none  [per_device(): sums = jnp.sum(lax.all_to_all(sends, ('dp', 'ctx'), 0, 0), axis=0)]
    all_to_all x1 -> x0, waiting for transfers between devices: 4.81 us -> none  [per_device(): sums = jnp.sum(lax.all_to_all(sends, ('dp', 'ctx'), 0, 0), axis=0)]
    pallas_call x2 -> x8, Pallas kernels: 12.5 us -> 7.94 us  [the longest x2 4.99 us: attend(): pl.pallas_call(functools.partial(attend_kernel, n_pieces, tok, bool(befor...]
    concatenate x4 -> x0, other arithmetic: 2.25 us -> none  [the longest x1 2.2 us: per_device(): jnp.concatenate(query_grads, axis=0)]
    another operation x2 -> x0, other arithmetic: 1.45 us -> none  [the longest x1 0.73 us: per_device(): value_grad = jnp.stack([g[1] for g in grads])]
  transfers between devices with their start and end apart: 11 -> 16, of which waited for: 5 -> 5; matrix products, arithmetic and copies ran while one was open for 7% -> 0% of each run, Pallas kernels for 19% -> 9%
where the time goes in v2:
time: 47.5 us; the launch traced here: 47.3 us
  starting transfers between devices  13.7 us (29%)
  blocking collectives  11.9 us (25%)
  waiting for transfers between devices  9.77 us (21%)
  Pallas kernels  7.94 us (17%)
  local copies, waits for them, and re-layouts  3.21 us (7%)
  between operations  0.71 us (1%)
    ppermute x16, starting transfers between devices, move(): return lax.ppermute(array, 'ctx', pairs)  13.7 us
    all_to_all x1, blocking collectives, step_device(): gathered = lax.all_to_all(shares, ('ctx', 'dp'), 0, 0)  11.9 us
    ppermute x16, waiting for transfers between devices, move(): return lax.ppermute(array, 'ctx', pairs)  9.77 us
    pallas_call x2, Pallas kernels, attend(): pl.pallas_call(functools.partial(attend_kernel, n_pieces, tok, bool(befor...  4.99 us
    unnamed x12, local copies, waits for them, and re-layouts  3.21 us
    pallas_call x1, Pallas kernels, join_q(): pl.pallas_call(functools.partial(join_q_kernel, docs), in_specs=[IN_SMEM]...  1.05 us
  transfers between devices with their start and end apart: 16, of which 5 were waited for; matrix products, arithmetic and copies ran while one was open for 0% of the time, Pallas kernels for 9%

profile of v2, /device:TPU:0, one launch (start us, length us, event | category | flops | bytes accessed | tf_op | source)
XLA Modules:
  0.0 47.3 jit_solution(4108222637750091731)
XLA Ops:
  0.6 0.0 copy-start.5
  0.6 0.0 copy-start.4
  0.7 0.7 %copy-done.5 = s32[2,64]{1,0:T(2,128)S(1)} copy-done((s32[2,64]{1,0:T(2,128)S(1)}, s32[2,64]{1,0:T(2,128)}, u32[]{:S(2)}) %copy-start.5) | copy-done | bytes 536
  1.3 0.0 copy-done.4
  1.3 0.0 copy-start
  1.3 1.2 %copy-done = bf16[2,64,4096]{2,1,0:T(8,128)(2,1)S(1)} copy-done((bf16[2,64,4096]{2,1,0:T(8,128)(2,1)S(1)}, bf16[2,64,4096]{2,1,0:T(8,128)(2,1)}, u32[]{:S(2)}) %copy-start) | copy-done | bytes 1048600
  2.6 0.0 copy-start.1
  2.6 1.2 %copy-done.1 = bf16[2,64,4096]{2,1,0:T(8,128)(2,1)S(1)} copy-done((bf16[2,64,4096]{2,1,0:T(8,128)(2,1)S(1)}, bf16[2,64,4096]{2,1,0:T(8,128)(2,1)}, u32[]{:S(2)}) %copy-start.1) | copy-done | bytes 1048600
  3.8 0.0 copy-start.2
  3.8 0.0 copy-start.3
  3.8 0.3 weigh.1
  4.1 0.6 %collective-permute-start = (bf16[2,64,2048]{2,1,0:T(8,128)(2,1)S(1)}, bf16[2,64,2048]{2,1,0:T(8,128)(2,1)S(1)}, u32[]{:S(2)}, u32[]{:S(2)}) collective-permute-start(bf16[2,64,2048]{2,1,0:T(8,128)(2,1)S(1)} %get-tuple-element.34), channel_id=1, source_target_pairs={{0,1},{1,0},{2,3},{3,2},{4,5},{5,4},{6,7},{7,6},{8,9},{9,8},{10,11... | collective-permute-start | bytes 1572872 | tf_op jit(solution)/shard_map/ppermute | solution.py:335
  4.7 0.1 collective-permute-start.5
  4.7 0.0 copy-done.2
  4.7 0.1 copy-done.3
  4.9 0.6 %collective-permute-start.1 = (bf16[2,64,512]{2,1,0:T(8,128)(2,1)S(1)}, bf16[2,64,512]{2,1,0:T(8,128)(2,1)S(1)}, u32[]{:S(2)}, u32[]{:S(2)}) collective-permute-start(bf16[2,64,512]{2,1,0:T(8,128)(2,1)S(1)} %get-tuple-element.36), channel_id=1, source_target_pairs={{0,1},{1,0},{2,3},{3,2},{4,5},{5,4},{6,7},{7,6},{8,9},{9,8},{10,11... | collective-permute-start | bytes 393224 | tf_op jit(solution)/shard_map/ppermute | solution.py:335
  5.4 2.6 %collective-permute-start.2 = (bf16[2,64,512]{2,1,0:T(8,128)(2,1)S(1)}, bf16[2,64,512]{2,1,0:T(8,128)(2,1)S(1)}, u32[]{:S(2)}, u32[]{:S(2)}) collective-permute-start(bf16[2,64,512]{2,1,0:T(8,128)(2,1)S(1)} %get-tuple-element.35.refs_0_), channel_id=1, source_target_pairs={{0,2},{1,3},{2,0},{3,1},{4,6},{5,7},{6,4},{7,5},{8,10},{9,11},{10,... | collective-permute-start | bytes 393224 | tf_op jit(solution)/shard_map/ppermute | solution.py:335
  8.0 0.0 collective-permute-start.3
  8.0 0.0 collective-permute-done.1.refs_1_
  8.0 0.2 collective-permute-start.6
  8.2 4.1 %collective-permute-done.2.refs_2_ = bf16[2,64,512]{2,1,0:T(8,128)(2,1)S(1)} collective-permute-done((bf16[2,64,512]{2,1,0:T(8,128)(2,1)S(1)}, bf16[2,64,512]{2,1,0:T(8,128)(2,1)S(1)}, u32[]{:S(2)}, u32[]{:S(2)}) %collective-permute-start.2) | collective-permute-done | bytes 131104 | tf_op jit(solution)/shard_map/ppermute | solution.py:335
  12.3 2.0 %collective-permute-start.7 = (bf16[2,64,512]{2,1,0:T(8,128)(2,1)S(1)}, bf16[2,64,512]{2,1,0:T(8,128)(2,1)S(1)}, u32[]{:S(2)}, u32[]{:S(2)}) collective-permute-start(bf16[2,64,512]{2,1,0:T(8,128)(2,1)S(1)} %get-tuple-element.41.refs_0_), channel_id=1, source_target_pairs={{0,2},{1,3},{2,0},{3,1},{4,6},{5,7},{6,4},{7,5},{8,10},{9,11},{10,... | collective-permute-start | bytes 393224 | tf_op jit(solution)/shard_map/ppermute | solution.py:335
  14.4 0.3 collective-permute-done.3.refs_3_
  14.7 1.9 %collective-permute-start.8 = (bf16[2,64,512]{2,1,0:T(8,128)(2,1)S(1)}, bf16[2,64,512]{2,1,0:T(8,128)(2,1)S(1)}, u32[]{:S(2)}, u32[]{:S(2)}) collective-permute-start(bf16[2,64,512]{2,1,0:T(8,128)(2,1)S(1)} %get-tuple-element.42), channel_id=1, source_target_pairs={{0,3},{1,2},{2,1},{3,0},{4,7},{5,6},{6,5},{7,4},{8,11},{9,10},{10,... | collective-permute-start | bytes 393224 | tf_op jit(solution)/shard_map/ppermute | solution.py:335
  16.6 0.0 collective-permute-done.swap_ref
  16.6 2.5 %attend.2 = (bf16[64,2048]{1,0:T(8,128)(2,1)S(1)}, bf16[64,2048]{1,0:T(8,128)(2,1)S(1)}, f32[16,128]{1,0:T(8,128)S(1)}, f32[4,256]{1,0:T(4,128)S(1)}, f32[2,64,5...) custom-call(bf16[2,64,2048]{2,1,0:T(8,128)(2,1)S(1)} %get-tuple-elem, ...), custom_call_target="tpu_custom_call" | custom-call | tf_op jit(solution)/shard_map/attend/pallas_call | solution.py:187
  19.1 0.0 collective-permute-done.6.refs_1_
  19.1 0.0 collective-permute-done.7.refs_2_
  19.1 1.2 %collective-permute-done.8.refs_3_ = bf16[2,64,512]{2,1,0:T(8,128)(2,1)S(1)} collective-permute-done((bf16[2,64,512]{2,1,0:T(8,128)(2,1)S(1)}, bf16[2,64,512]{2,1,0:T(8,128)(2,1)S(1)}, u32[]{:S(2)}, u32[]{:S(2)}) %collective-permute-start.8) | collective-permute-done | bytes 131104 | tf_op jit(solution)/shard_map/ppermute | solution.py:335
  20.4 0.0 collective-permute-done.5.swap_ref
  20.4 2.5 %attend.3 = (bf16[64,2048]{1,0:T(8,128)(2,1)S(1)}, bf16[64,2048]{1,0:T(8,128)(2,1)S(1)}, f32[16,128]{1,0:T(8,128)S(1)}, f32[4,256]{1,0:T(4,128)S(1)}, f32[2,64,5...) custom-call(bf16[2,64,2048]{2,1,0:T(8,128)(2,1)S(1)} %get-tuple-elem, ...), custom_call_target="tpu_custom_call" | custom-call | tf_op jit(solution)/shard_map/attend/pallas_call | solution.py:187
  22.8 1.2 %collective-permute-start.13 = (bf16[2,64,512]{2,1,0:T(8,128)(2,1)S(1)}, bf16[2,64,512]{2,1,0:T(8,128)(2,1)S(1)}, u32[]{:S(2)}, u32[]{:S(2)}) collective-permute-start(bf16[2,64,512]{2,1,0:T(8,128)(2,1)S(1)} %get-tuple-element.52), channel_id=1, source_target_pairs={{0,2},{1,3},{2,0},{3,1},{4,6},{5,7},{6,4},{7,5},{8,10},{9,11},{10,... | collective-permute-start | bytes 393224 | tf_op jit(solution)/shard_map/ppermute | solution.py:335
  24.1 0.3 collective-permute-start.14
  24.4 0.7 %collective-permute-start.15 = (bf16[2,64,512]{2,1,0:T(8,128)(2,1)S(1)}, bf16[2,64,512]{2,1,0:T(8,128)(2,1)S(1)}, u32[]{:S(2)}, u32[]{:S(2)}) collective-permute-start(bf16[2,64,512]{2,1,0:T(8,128)(2,1)S(1)} %get-tuple-element.54), channel_id=1, source_target_pairs={{0,3},{1,2},{2,1},{3,0},{4,7},{5,6},{6,5},{7,4},{8,11},{9,10},{10,... | collective-permute-start | bytes 393224 | tf_op jit(solution)/shard_map/ppermute | solution.py:335
  25.1 0.0 collective-permute-start.9
  25.1 0.5 %collective-permute-start.4 = (bf16[64,2048]{1,0:T(8,128)(2,1)S(1)}, bf16[64,2048]{1,0:T(8,128)(2,1)S(1)}, u32[]{:S(2)}, u32[]{:S(2)}) collective-permute-start(bf16[64,2048]{1,0:T(8,128)(2,1)S(1)} %get-tuple-element.38), channel_id=1, source_target_pairs={{0,1},{1,0},{2,3},{3,2},{4,5},{5,4},{6,7},{7,6},{8,9},{9,8},{10,11... | collective-permute-start | bytes 786440 | tf_op jit(solution)/shard_map/ppermute | solution.py:335
  25.6 3.7 %collective-permute-done.13.refs_5_ = bf16[2,64,512]{2,1,0:T(8,128)(2,1)S(1)} collective-permute-done((bf16[2,64,512]{2,1,0:T(8,128)(2,1)S(1)}, bf16[2,64,512]{2,1,0:T(8,128)(2,1)S(1)}, u32[]{:S(2)}, u32[]{:S(2)}) %collective-permute-start.13) | collective-permute-done | bytes 131104 | tf_op jit(solution)/shard_map/ppermute | solution.py:335
  29.3 1.2 %collective-permute-start.10 = (bf16[2,64,512]{2,1,0:T(8,128)(2,1)S(1)}, bf16[2,64,512]{2,1,0:T(8,128)(2,1)S(1)}, u32[]{:S(2)}, u32[]{:S(2)}) collective-permute-start(bf16[2,64,512]{2,1,0:T(8,128)(2,1)S(1)} %get-tuple-element.48), channel_id=1, source_target_pairs={{0,2},{1,3},{2,0},{3,1},{4,6},{5,7},{6,4},{7,5},{8,10},{9,11},{10,... | collective-permute-start | bytes 393224 | tf_op jit(solution)/shard_map/ppermute | solution.py:335
  30.5 0.0 collective-permute-done.14.refs_6_
  30.5 0.0 collective-permute-start.11
  30.5 0.3 collective-permute-done.15.refs_7_
  30.8 1.9 %collective-permute-start.12 = (bf16[2,64,512]{2,1,0:T(8,128)(2,1)S(1)}, bf16[2,64,512]{2,1,0:T(8,128)(2,1)S(1)}, u32[]{:S(2)}, u32[]{:S(2)}) collective-permute-start(bf16[2,64,512]{2,1,0:T(8,128)(2,1)S(1)} %get-tuple-element.50), channel_id=1, source_target_pairs={{0,3},{1,2},{2,1},{3,0},{4,7},{5,6},{6,5},{7,4},{8,11},{9,10},{10,... | collective-permute-start | bytes 393224 | tf_op jit(solution)/shard_map/ppermute | solution.py:335
  32.7 11.9 %all_to_all.5.gathered_ref = f32[32,1,384]{2,1,0:T(1,128)S(1)} all-to-all(f32[32,1,384]{2,1,0:T(1,128)S(1)} %share.1), channel_id=1, replica_groups=mesh['dp'=8,'ctx'=4] {'ctx','dp'}, dimensions={0} | all-to-all | bytes 98304 | tf_op jit(solution)/shard_map/all_to_all | solution.py:357
  44.7 0.6 %bias_out.1 = (f32[1,128]{1,0:T(1,128)}, f32[2,128]{1,0:T(2,128)}) custom-call(f32[32,1,384]{2,1,0:T(1,128)S(1)} %all_to_all.5.gathered_ref), custom_call_target="tpu_custom_call" | custom-call | tf_op jit(solution)/shard_map/bias_out/pallas_call | solution.py:309
  45.3 0.0 collective-permute-done.10.refs_1_
  45.3 0.0 collective-permute-done.11.refs_2_
  45.3 0.0 collective-permute-done.12.refs_3_
  45.3 0.9 %join_kv.1 = (bf16[2,64,1024]{2,1,0:T(8,128)(2,1)}, bf16[2,64,1024]{2,1,0:T(8,128)(2,1)}) custom-call(s32[1]{0:T(128)} %bitcast.place_ref, f32[2,64,512]{2,1,0:T(8,128)S(1)} %get-tuple-element.47.refs_0_, bf16[2,64,512]{2,1,0:T(8,128)(2,1)S(1)} %collective-permute-done.10.refs_1_, bf16[2,64,512]{2,1,0:T(8,128)(2,1)S(1)} %collective-permute-done.11.refs_2_, ...), custom_call_target="tpu_custom_call" | custom-call | tf_op jit(solution)/shard_map/join_kv/pallas_call | solution.py:292
  46.2 0.0 collective-permute-done.9.refs_3_
  46.2 0.0 collective-permute-done.4.refs_1_
  46.2 1.0 %join_q.1 = bf16[2,64,4096]{2,1,0:T(8,128)(2,1)} custom-call(s32[1]{0:T(128)} %bitcast.place_ref, bf16[64,2048]{1,0:T(8,128)(2,1)S(1)} %get-tuple-element.37.refs_0_, bf16[64,2048]{1,0:T(8,128)(2,1)S(1)} %collective-permute-done.4.refs_1_, bf16[64,2048]{1,0:T(8,128)(2,1)S(1)} %get-tuple-element.45.refs_2_, bf16[64,2048]{1,0:T(8,128)(2,1)S(1)} %collective-permute-done.9.refs_3_), custom_call_target="tpu_custom_call" | custom-call | tf_op jit(solution)/shard_map/join_q/pallas_call | solution.py:262
  (2 shorter events, 0.1 us)
Async XLA Ops:
  0.6 0.7 %copy-start.5 = (s32[2,64]{1,0:T(2,128)S(1)}, s32[2,64]{1,0:T(2,128)}, u32[]{:S(2)}) copy-start(s32[2,64]{1,0:T(2,128)} %bucket_ref.1) | copy-start | bytes 1540
  0.6 0.7 %copy-start.4 = (s32[2,128]{1,0:T(2,128)S(1)}, s32[2,128]{1,0:T(2,128)}, u32[]{:S(2)}) copy-start(s32[2,128]{1,0:T(2,128)} %masked_ref.1) | copy-start | bytes 3076
  1.3 1.2 %copy-start = (bf16[2,64,4096]{2,1,0:T(8,128)(2,1)S(1)}, bf16[2,64,4096]{2,1,0:T(8,128)(2,1)}, u32[]{:S(2)}) copy-start(bf16[2,64,4096]{2,1,0:T(8,128)(2,1)} %query_ref.1) | copy-start | bytes 3145732
  2.6 1.2 %copy-start.1 = (bf16[2,64,4096]{2,1,0:T(8,128)(2,1)S(1)}, bf16[2,64,4096]{2,1,0:T(8,128)(2,1)}, u32[]{:S(2)}) copy-start(bf16[2,64,4096]{2,1,0:T(8,128)(2,1)} %grad_ref.1) | copy-start | bytes 3145732
  3.8 1.0 %copy-start.2 = (bf16[2,64,1024]{2,1,0:T(8,128)(2,1)S(1)}, bf16[2,64,1024]{2,1,0:T(8,128)(2,1)}, u32[]{:S(2)}) copy-start(bf16[2,64,1024]{2,1,0:T(8,128)(2,1)} %key_other.1) | copy-start | bytes 786436
  3.8 1.0 %copy-start.3 = (bf16[2,64,1024]{2,1,0:T(8,128)(2,1)S(1)}, bf16[2,64,1024]{2,1,0:T(8,128)(2,1)}, u32[]{:S(2)}) copy-start(bf16[2,64,1024]{2,1,0:T(8,128)(2,1)} %value_other.1) | copy-start | bytes 786436
  4.1 12.5 %collective-permute-start = (bf16[2,64,2048]{2,1,0:T(8,128)(2,1)S(1)}, bf16[2,64,2048]{2,1,0:T(8,128)(2,1)S(1)}, u32[]{:S(2)}, u32[]{:S(2)}) collective-permute-start(bf16[2,64,2048]{2,1,0:T(8,128)(2,1)S(1)} %get-tuple-element.34), channel_id=1, source_target_pairs={{0,1},{1,0},{2,3},{3,2},{4,5},{5,4},{6,7},{7,6},{8,9},{9,8},{10,11... | collective-permute-start | bytes 1572872 | tf_op jit(solution)/shard_map/ppermute | solution.py:335
  4.7 15.7 %collective-permute-start.5 = (bf16[2,64,2048]{2,1,0:T(8,128)(2,1)S(1)}, bf16[2,64,2048]{2,1,0:T(8,128)(2,1)S(1)}, u32[]{:S(2)}, u32[]{:S(2)}) collective-permute-start(bf16[2,64,2048]{2,1,0:T(8,128)(2,1)S(1)} %get-tuple-element.40), channel_id=1, source_target_pairs={{0,1},{1,0},{2,3},{3,2},{4,5},{5,4},{6,7},{7,6},{8,9},{9,8},{10,11... | collective-permute-start | bytes 1572872 | tf_op jit(solution)/shard_map/ppermute | solution.py:335
  4.9 3.2 %collective-permute-start.1 = (bf16[2,64,512]{2,1,0:T(8,128)(2,1)S(1)}, bf16[2,64,512]{2,1,0:T(8,128)(2,1)S(1)}, u32[]{:S(2)}, u32[]{:S(2)}) collective-permute-start(bf16[2,64,512]{2,1,0:T(8,128)(2,1)S(1)} %get-tuple-element.36), channel_id=1, source_target_pairs={{0,1},{1,0},{2,3},{3,2},{4,5},{5,4},{6,7},{7,6},{8,9},{9,8},{10,11... | collective-permute-start | bytes 393224 | tf_op jit(solution)/shard_map/ppermute | solution.py:335
  5.4 6.9 %collective-permute-start.2 = (bf16[2,64,512]{2,1,0:T(8,128)(2,1)S(1)}, bf16[2,64,512]{2,1,0:T(8,128)(2,1)S(1)}, u32[]{:S(2)}, u32[]{:S(2)}) collective-permute-start(bf16[2,64,512]{2,1,0:T(8,128)(2,1)S(1)} %get-tuple-element.35.refs_0_), channel_id=1, source_target_pairs={{0,2},{1,3},{2,0},{3,1},{4,6},{5,7},{6,4},{7,5},{8,10},{9,11},{10,... | collective-permute-start | bytes 393224 | tf_op jit(solution)/shard_map/ppermute | solution.py:335
  8.0 6.7 %collective-permute-start.3 = (bf16[2,64,512]{2,1,0:T(8,128)(2,1)S(1)}, bf16[2,64,512]{2,1,0:T(8,128)(2,1)S(1)}, u32[]{:S(2)}, u32[]{:S(2)}) collective-permute-start(bf16[2,64,512]{2,1,0:T(8,128)(2,1)S(1)} %get-tuple-element.36), channel_id=1, source_target_pairs={{0,3},{1,2},{2,1},{3,0},{4,7},{5,6},{6,5},{7,4},{8,11},{9,10},{10,... | collective-permute-start | bytes 393224 | tf_op jit(solution)/shard_map/ppermute | solution.py:335
  8.0 11.1 %collective-permute-start.6 = (bf16[2,64,512]{2,1,0:T(8,128)(2,1)S(1)}, bf16[2,64,512]{2,1,0:T(8,128)(2,1)S(1)}, u32[]{:S(2)}, u32[]{:S(2)}) collective-permute-start(bf16[2,64,512]{2,1,0:T(8,128)(2,1)S(1)} %get-tuple-element.42), channel_id=1, source_target_pairs={{0,1},{1,0},{2,3},{3,2},{4,5},{5,4},{6,7},{7,6},{8,9},{9,8},{10,11... | collective-permute-start | bytes 393224 | tf_op jit(solution)/shard_map/ppermute | solution.py:335
  12.3 6.8 %collective-permute-start.7 = (bf16[2,64,512]{2,1,0:T(8,128)(2,1)S(1)}, bf16[2,64,512]{2,1,0:T(8,128)(2,1)S(1)}, u32[]{:S(2)}, u32[]{:S(2)}) collective-permute-start(bf16[2,64,512]{2,1,0:T(8,128)(2,1)S(1)} %get-tuple-element.41.refs_0_), channel_id=1, source_target_pairs={{0,2},{1,3},{2,0},{3,1},{4,6},{5,7},{6,4},{7,5},{8,10},{9,11},{10,... | collective-permute-start | bytes 393224 | tf_op jit(solution)/shard_map/ppermute | solution.py:335
  14.7 5.7 %collective-permute-start.8 = (bf16[2,64,512]{2,1,0:T(8,128)(2,1)S(1)}, bf16[2,64,512]{2,1,0:T(8,128)(2,1)S(1)}, u32[]{:S(2)}, u32[]{:S(2)}) collective-permute-start(bf16[2,64,512]{2,1,0:T(8,128)(2,1)S(1)} %get-tuple-element.42), channel_id=1, source_target_pairs={{0,3},{1,2},{2,1},{3,0},{4,7},{5,6},{6,5},{7,4},{8,11},{9,10},{10,... | collective-permute-start | bytes 393224 | tf_op jit(solution)/shard_map/ppermute | solution.py:335
  22.8 6.4 %collective-permute-start.13 = (bf16[2,64,512]{2,1,0:T(8,128)(2,1)S(1)}, bf16[2,64,512]{2,1,0:T(8,128)(2,1)S(1)}, u32[]{:S(2)}, u32[]{:S(2)}) collective-permute-start(bf16[2,64,512]{2,1,0:T(8,128)(2,1)S(1)} %get-tuple-element.52), channel_id=1, source_target_pairs={{0,2},{1,3},{2,0},{3,1},{4,6},{5,7},{6,4},{7,5},{8,10},{9,11},{10,... | collective-permute-start | bytes 393224 | tf_op jit(solution)/shard_map/ppermute | solution.py:335
  24.1 6.4 %collective-permute-start.14 = (bf16[2,64,512]{2,1,0:T(8,128)(2,1)S(1)}, bf16[2,64,512]{2,1,0:T(8,128)(2,1)S(1)}, u32[]{:S(2)}, u32[]{:S(2)}) collective-permute-start(bf16[2,64,512]{2,1,0:T(8,128)(2,1)S(1)} %get-tuple-element.53), channel_id=1, source_target_pairs={{0,1},{1,0},{2,3},{3,2},{4,5},{5,4},{6,7},{7,6},{8,9},{9,8},{10,11... | collective-permute-start | bytes 393224 | tf_op jit(solution)/shard_map/ppermute | solution.py:335
  24.4 6.4 %collective-permute-start.15 = (bf16[2,64,512]{2,1,0:T(8,128)(2,1)S(1)}, bf16[2,64,512]{2,1,0:T(8,128)(2,1)S(1)}, u32[]{:S(2)}, u32[]{:S(2)}) collective-permute-start(bf16[2,64,512]{2,1,0:T(8,128)(2,1)S(1)} %get-tuple-element.54), channel_id=1, source_target_pairs={{0,3},{1,2},{2,1},{3,0},{4,7},{5,6},{6,5},{7,4},{8,11},{9,10},{10,... | collective-permute-start | bytes 393224 | tf_op jit(solution)/shard_map/ppermute | solution.py:335
  25.1 21.2 %collective-permute-start.9 = (bf16[64,2048]{1,0:T(8,128)(2,1)S(1)}, bf16[64,2048]{1,0:T(8,128)(2,1)S(1)}, u32[]{:S(2)}, u32[]{:S(2)}) collective-permute-start(bf16[64,2048]{1,0:T(8,128)(2,1)S(1)} %get-tuple-element.46), channel_id=1, source_target_pairs={{0,1},{1,0},{2,3},{3,2},{4,5},{5,4},{6,7},{7,6},{8,9},{9,8},{10,11... | collective-permute-start | bytes 786440 | tf_op jit(solution)/shard_map/ppermute | solution.py:335
  25.1 21.2 %collective-permute-start.4 = (bf16[64,2048]{1,0:T(8,128)(2,1)S(1)}, bf16[64,2048]{1,0:T(8,128)(2,1)S(1)}, u32[]{:S(2)}, u32[]{:S(2)}) collective-permute-start(bf16[64,2048]{1,0:T(8,128)(2,1)S(1)} %get-tuple-element.38), channel_id=1, source_target_pairs={{0,1},{1,0},{2,3},{3,2},{4,5},{5,4},{6,7},{7,6},{8,9},{9,8},{10,11... | collective-permute-start | bytes 786440 | tf_op jit(solution)/shard_map/ppermute | solution.py:335
  29.3 16.0 %collective-permute-start.10 = (bf16[2,64,512]{2,1,0:T(8,128)(2,1)S(1)}, bf16[2,64,512]{2,1,0:T(8,128)(2,1)S(1)}, u32[]{:S(2)}, u32[]{:S(2)}) collective-permute-start(bf16[2,64,512]{2,1,0:T(8,128)(2,1)S(1)} %get-tuple-element.48), channel_id=1, source_target_pairs={{0,2},{1,3},{2,0},{3,1},{4,6},{5,7},{6,4},{7,5},{8,10},{9,11},{10,... | collective-permute-start | bytes 393224 | tf_op jit(solution)/shard_map/ppermute | solution.py:335
  30.5 14.8 %collective-permute-start.11 = (bf16[2,64,512]{2,1,0:T(8,128)(2,1)S(1)}, bf16[2,64,512]{2,1,0:T(8,128)(2,1)S(1)}, u32[]{:S(2)}, u32[]{:S(2)}) collective-permute-start(bf16[2,64,512]{2,1,0:T(8,128)(2,1)S(1)} %get-tuple-element.49), channel_id=1, source_target_pairs={{0,1},{1,0},{2,3},{3,2},{4,5},{5,4},{6,7},{7,6},{8,9},{9,8},{10,11... | collective-permute-start | bytes 393224 | tf_op jit(solution)/shard_map/ppermute | solution.py:335
  30.8 14.5 %collective-permute-start.12 = (bf16[2,64,512]{2,1,0:T(8,128)(2,1)S(1)}, bf16[2,64,512]{2,1,0:T(8,128)(2,1)S(1)}, u32[]{:S(2)}, u32[]{:S(2)}) collective-permute-start(bf16[2,64,512]{2,1,0:T(8,128)(2,1)S(1)} %get-tuple-element.50), channel_id=1, source_target_pairs={{0,3},{1,2},{2,1},{3,0},{4,7},{5,6},{6,5},{7,4},{8,11},{9,10},{10,... | collective-permute-start | bytes 393224 | tf_op jit(solution)/shard_map/ppermute | solution.py:335

commit v3 on v2

v3 whole, which is shorter than its diff:
```python
import functools
import math

import jax
import jax.numpy as jnp
from jax import lax
from jax.experimental import pallas as pl
from jax.experimental.pallas import tpu as pltpu
from jax.sharding import PartitionSpec as P


H = 32
KVH = 8
HD = 128
NB = 16
GROUP = H // KVH
CORES = 2
HEADS = KVH // CORES
QW = HEADS * GROUP * HD
KW = HEADS * HD

NT = (((1,), (1,)), ((), ()))
NN = (((1,), (0,)), ((), ()))
TN = (((0,), (0,)), ((), ()))
BF = jnp.bfloat16
F32 = jnp.float32


def dot(a, b, dims):
    return lax.dot_general(a, b, dims, preferred_element_type=F32)


def whole(shape):
    return pl.BlockSpec(shape, lambda *_: (0,) * len(shape))


HELD_CTX = 4


def fits(n_ctx):
    return n_ctx <= HELD_CTX


def vmem(shape, dtype):
    if fits(lax.axis_size("ctx")):
        return pltpu.VMEM(shape, dtype)
    return jax.ShapeDtypeStruct(shape, dtype)


def held(array):
    if fits(lax.axis_size("ctx")):
        return pltpu.with_memory_space_constraint(array, pltpu.VMEM)
    return array


def in_hbm(array):
    if fits(lax.axis_size("ctx")):
        return pltpu.with_memory_space_constraint(array, pltpu.HBM)
    return array


def grant(mib):
    if fits(lax.axis_size("ctx")):
        return pltpu.CompilerParams(vmem_limit_bytes=mib << 20)
    return None


IN_VMEM = pl.BlockSpec(memory_space=pltpu.VMEM)
IN_SMEM = pl.BlockSpec(memory_space=pltpu.SMEM)


def chunks_of(docs):
    mid = HEADS // 2
    return [(d, 0, HEADS) for d in range(docs - 1)] + [(docs - 1, 0, mid), (docs - 1, mid, HEADS)]


def returns_of(docs):
    last = len(chunks_of(docs)) - 1
    return [[n] for n in range(last - 2)] + [[last - 2, last - 1], [last]]


def split_kv_kernel(chunks, place_ref, key_ref, value_ref, *refs):
    outs, sems = refs[:-1], refs[-1]
    core = place_ref[0] % CORES
    copies = []
    for n, (d, lo, hi) in enumerate(chunks):
        for side, half in ((0, core), (1, 1 - core)):
            start = pl.multiple_of(half * KW + lo * HD, HD)
            for which, ref in ((0, key_ref), (1, value_ref)):
                copies.append(
                    pltpu.make_async_copy(
                        ref.at[d, :, pl.ds(start, (hi - lo) * HD)],
                        outs[2 * n + side].at[which],
                        sems.at[len(copies)],
                    )
                )
    for copy in copies:
        copy.start()
    for copy in copies:
        copy.wait()


def split_kv(place, key_in, value_in):
    docs, tok = key_in.shape[:2]
    chunks = chunks_of(docs)
    shapes = [(2, tok, (hi - lo) * HD) for _, lo, hi in chunks for _ in range(2)]
    outs = pl.pallas_call(
        functools.partial(split_kv_kernel, chunks),
        in_specs=[IN_SMEM, pl.BlockSpec(memory_space=pl.ANY), pl.BlockSpec(memory_space=pl.ANY)],
        out_specs=[IN_VMEM] * len(shapes),
        out_shape=[vmem(shape, BF) for shape in shapes],
        scratch_shapes=[pltpu.SemaphoreType.DMA((2 * len(shapes),))],
        compiler_params=grant(4),
        name="split_kv",
    )(place, in_hbm(key_in), in_hbm(value_in))
    return outs[0::2], outs[1::2]


def weigh_kernel(
    place_ref, masked_ref, bucket_ref, query_own, grad_own, query_ref, grad_ref, *outs
):
    docs, tok = query_ref.shape[:2]
    rows = lax.broadcasted_iota(jnp.int32, (tok, masked_ref.shape[1]), 0) + place_ref[0] * tok
    lane = lax.broadcasted_iota(jnp.int32, (tok, tok), 1)
    line = lax.broadcasted_iota(jnp.int32, (tok, tok), 0)
    for d in range(docs):
        hit = jnp.where(masked_ref[d : d + 1, :] == rows, 1.0, 0.0)
        is_masked = jnp.max(hit, axis=1, keepdims=True)
        spread = jnp.where(lane == line, bucket_ref[d : d + 1, :].astype(F32), 0.0)
        level = jnp.sum(spread, axis=1, keepdims=True)
        weight = is_masked * NB / (level + 1.0)
        outs[2 * d][0] = query_own[d]
        outs[2 * d][1] = (grad_own[d].astype(F32) * weight).astype(BF)
        outs[2 * d + 1][0] = query_ref[d]
        outs[2 * d + 1][1] = (grad_ref[d].astype(F32) * weight).astype(BF)


def weigh(place, masked, bucket, query, out_grad):
    docs, tok = query.shape[:2]
    own = pl.BlockSpec((docs, tok, QW), lambda g, p: (0, 0, p[0] % CORES))
    other = pl.BlockSpec((docs, tok, QW), lambda g, p: (0, 0, 1 - p[0] % CORES))
    outs = pl.pallas_call(
        weigh_kernel,
        grid_spec=pltpu.PrefetchScalarGridSpec(
            num_scalar_prefetch=1,
            grid=(1,),
            in_specs=[whole(masked.shape), whole(bucket.shape), own, own, other, other],
            out_specs=[IN_VMEM] * (2 * docs),
        ),
        out_shape=[vmem((2, tok, QW), BF)] * (2 * docs),
        compiler_params=grant(8),
        name="weigh",
    )(place, masked, bucket, *[in_hbm(a) for a in (query, out_grad, query, out_grad)])
    return outs[0::2], outs[1::2]


def attend_kernel(n_pieces, tok, lo, hi, skip, before, n_dp, place_ref, own_ref, swap_ref, *refs):
    piece_refs, refs = refs[:n_pieces], refs[n_pieces:]
    if skip:
        carry_refs, refs = refs[:n_pieces], refs[n_pieces:]
    before_refs, refs = refs[: 2 * len(before)], refs[2 * len(before) :]
    dq_ref, dq_sib_ref, *refs = refs
    qsum_ref, kvsum_ref, near_ref, *far_refs = refs
    inv_root = 1.0 / math.sqrt(HD)
    if skip:
        dq_sib_ref[:, : skip * GROUP * HD] = carry_refs[0][...]
        for far_ref, carry_ref in zip(far_refs, carry_refs[1:]):
            far_ref[:, :, : skip * HD] = carry_ref[...]
    for g in range(lo, hi):
        cols = [slice((g * GROUP + h) * HD, (g * GROUP + h + 1) * HD) for h in range(GROUP)]
        kv = slice((g - lo) * HD, (g - lo + 1) * HD)
        kv_out = slice((g - lo + skip) * HD, (g - lo + skip + 1) * HD)
        q_rows, c_rows = (
            jnp.concatenate([ref[which, :, c] for ref in (own_ref, swap_ref) for c in cols], axis=0)
            for which in (0, 1)
        )
        keys, values = (
            jnp.concatenate([r[which, :, kv] for r in piece_refs], axis=0) for which in (0, 1)
        )
        scores = dot(keys, q_rows, NT)
        prob_grad = dot(values, c_rows, NT)
        top = jnp.max(scores, axis=0, keepdims=True)
        expo = jnp.exp((scores - top) * inv_root)
        probs = expo * (1.0 / jnp.sum(expo, axis=0, keepdims=True))
        low = probs.astype(BF)
        delta = jnp.sum(low.astype(F32) * prob_grad, axis=0, keepdims=True)
        score_low = (probs * (prob_grad - delta) * inv_root).astype(BF)
        dv = dot(low, c_rows, NN)
        dk = dot(score_low, q_rows, NN)
        dq = dot(score_low, keys, TN)
        for h in range(GROUP):
            row = (g - lo) * GROUP + h
            c = slice(row * HD, (row + 1) * HD)
            part = dq[h * tok : (h + 1) * tok]
            other = dq[(GROUP + h) * tok : (GROUP + h + 1) * tok]
            dq_ref[:, c] = part.astype(BF)
            out = row + skip * GROUP
            dq_sib_ref[:, out * HD : (out + 1) * HD] = other.astype(BF)
            qsum_ref[row : row + 1] = jnp.sum(part + other, axis=0, keepdims=True)
        for which, full in ((0, dk), (1, dv)):
            side = slice(which * HD, (which + 1) * HD)
            kvsum_ref[g - lo : g - lo + 1, side] = jnp.sum(full, axis=0, keepdims=True)
            near_ref[which, :, kv] = full[:tok]
            for piece in range(1, n_pieces):
                part = full[piece * tok : (piece + 1) * tok]
                far_refs[piece - 1][which, :, kv_out] = part.astype(BF)
    if before:
        share_ref = far_refs[n_pieces - 1]
        sums = [(lo, hi, qsum_ref, kvsum_ref)]
        sums += [(a, b, *before_refs[2 * i : 2 * i + 2]) for i, (a, b) in enumerate(before)]
        core = place_ref[0] % CORES
        share_ref[...] = jnp.zeros(share_ref.shape, F32)
        for g in range(HEADS):
            here = [(g - a, q, kv) for a, b, q, kv in sums if a <= g < b]
            for h in range(GROUP):
                rows = [q[i * GROUP + h : i * GROUP + h + 1] for i, q, _ in here]
                share_ref[core * (HEADS * GROUP) + g * GROUP + h, :, :HD] = sum(rows[1:], rows[0])
            rows = [kv[i : i + 1] for i, _, kv in here]
            total = sum(rows[1:], rows[0])
            for c in range(share_ref.shape[0] // n_dp):
                share_ref[c * n_dp + core * HEADS + g, :, HD:] = total


def attend(place, own, swap, pieces, lo, hi, carry, before, ranges, n_dp, rows):
    tok = own.shape[1]
    n_pieces = len(pieces)
    heads = hi - lo
    skip = carry[1].shape[2] // HD if carry else 0
    args = [own, swap, *pieces, *carry, *[part for pair in before for part in pair]]
    out_shape = [
        vmem((tok, heads * GROUP * HD), BF),
        vmem((tok, (heads + skip) * GROUP * HD), BF),
        vmem((heads * GROUP, HD), F32),
        vmem((heads, 2 * HD), F32),
        vmem((2, tok, heads * HD), F32),
        *[vmem((2, tok, (heads + skip) * HD), BF)] * (n_pieces - 1),
    ]
    if before:
        out_shape.append(jax.ShapeDtypeStruct((rows, 1, 3 * HD), F32))
    ranges = ranges if before else []
    outs = pl.pallas_call(
        functools.partial(attend_kernel, n_pieces, tok, lo, hi, skip, ranges, n_dp),
        in_specs=[IN_SMEM] + [IN_VMEM] * len(args),
        out_specs=[IN_VMEM] * len(out_shape),
        out_shape=out_shape,
        compiler_params=grant(20),
        name="attend",
    )(place, *[held(arg) for arg in args])
    return outs[:2], outs[2:4], outs[4], outs[5 : 4 + n_pieces], outs[-1]


def shares_of(place, sums, chunks, n_ctx, n_dp):
    q_w = H * HD // (n_ctx * n_dp)
    p_w = KVH * HD // n_dp
    core = place[0] % CORES
    qsum = jnp.zeros((HEADS * GROUP, HD), F32)
    kvsum = jnp.zeros((HEADS, 2 * HD), F32)
    for (_, lo, hi), (q, kv) in zip(chunks, sums):
        qsum = qsum.at[lo * GROUP : hi * GROUP].add(q)
        kvsum = kvsum.at[lo:hi].add(kv)

    def both_halves(part):
        return jnp.concatenate([jnp.where(core == c, part, 0.0) for c in range(CORES)], axis=0)

    q_part = both_halves(qsum).reshape(n_ctx, n_dp, q_w)
    pair = both_halves(kvsum)
    pair = jnp.concatenate(
        [pair[:, :HD].reshape(n_dp, p_w), pair[:, HD:].reshape(n_dp, p_w)], axis=1
    )
    pair = jnp.broadcast_to(pair[None], (n_ctx, n_dp, 2 * p_w))
    return jnp.concatenate([q_part, pair], axis=-1).reshape(n_ctx * n_dp, 1, q_w + 2 * p_w)


def place_of(n, docs):
    chunks = chunks_of(docs)
    for i, group in enumerate(returns_of(docs)):
        if n in group:
            ahead = group[: group.index(n)]
            return i, sum(chunks[m][2] - chunks[m][1] for m in ahead)


def join_q_kernel(docs, place_ref, *refs):
    chunks = chunks_of(docs)
    out_ref, near_refs, far_refs = refs[-1], refs[: len(chunks)], refs[len(chunks) : -1]
    width = GROUP * HD
    for core in range(CORES):

        @pl.when(place_ref[0] % CORES == core)
        def _():
            for n, (d, lo, hi) in enumerate(chunks):
                mine, other = (half * HEADS + lo for half in (core, 1 - core))
                i, ahead = place_of(n, docs)
                heads = hi - lo
                out_ref[d, :, mine * width : (mine + heads) * width] = near_refs[n][...]
                out_ref[d, :, other * width : (other + heads) * width] = far_refs[i][
                    :, ahead * width : (ahead + heads) * width
                ]


def join_q(place, near, far, docs):
    tok = near[0].shape[0]
    args = near + far
    return pl.pallas_call(
        functools.partial(join_q_kernel, docs),
        in_specs=[IN_SMEM] + [IN_VMEM] * len(args),
        out_shape=jax.ShapeDtypeStruct((docs, tok, CORES * QW), BF),
        compiler_params=grant(6),
        name="join_q",
    )(place, *[held(arg) for arg in args])


def join_kv_kernel(docs, chips, place_ref, *refs):
    chunks = chunks_of(docs)
    *refs, key_ref, value_ref = refs
    near_refs, back_refs = refs[: len(chunks)], refs[len(chunks) :]
    per_group = CORES * chips - 1
    for core in range(CORES):

        @pl.when(place_ref[0] % CORES == core)
        def _():
            for n, (d, lo, hi) in enumerate(chunks):
                i, ahead = place_of(n, docs)
                cols = slice(ahead * HD, (ahead + hi - lo) * HD)
                back = back_refs[i * per_group : (i + 1) * per_group]
                hops = hops_of(CORES * chips)
                for side, half in ((0, core), (1, 1 - core)):
                    terms = [ref[:, :, cols].astype(F32) for ref, (_, x) in zip(back, hops) if x == side]
                    if side == 0:
                        terms.append(near_refs[n][...])
                    total = sum(terms[1:], terms[0])
                    out = slice((half * HEADS + lo) * HD, (half * HEADS + hi) * HD)
                    key_ref[d, :, out] = total[0].astype(BF)
                    value_ref[d, :, out] = total[1].astype(BF)


def join_kv(place, near, back, docs, chips):
    tok = near[0].shape[1]
    shape = jax.ShapeDtypeStruct((docs, tok, CORES * KW), BF)
    args = near + [part for group in back for part in group]
    return pl.pallas_call(
        functools.partial(join_kv_kernel, docs, chips),
        in_specs=[IN_SMEM] + [IN_VMEM] * len(args),
        out_shape=[shape, shape],
        compiler_params=grant(6),
        name="join_kv",
    )(place, *[held(arg) for arg in args])


def bias_kernel(norm_factor, gathered_ref, query_ref, pair_ref):
    q_w, p_w = query_ref.shape[1], pair_ref.shape[1]
    totals = jnp.sum(gathered_ref[...], axis=0) * norm_factor
    query_ref[...] = totals[:, :q_w]
    pair_ref[0:1] = totals[:, q_w : q_w + p_w]
    pair_ref[1:2] = totals[:, q_w + p_w :]


def bias_out(gathered, norm_factor, q_w, p_w):
    return pl.pallas_call(
        functools.partial(bias_kernel, norm_factor),
        in_specs=[IN_VMEM],
        out_shape=[
            jax.ShapeDtypeStruct((1, q_w), F32),
            jax.ShapeDtypeStruct((2, p_w), F32),
        ],
        compiler_params=grant(2),
        name="bias_out",
    )(held(gathered))


def hops_of(n_ctx):
    return [(s, x) for s in range(1, n_ctx // CORES) for x in range(CORES)] + [(0, 1)]


def step_device(query, key_in, value_in, out_grad, masked, bucket):
    n_ctx = lax.axis_size("ctx")
    n_dp = lax.axis_size("dp")
    docs, tok = query.shape[:2]
    chips = n_ctx // CORES
    hops = hops_of(n_ctx)
    chunks = chunks_of(docs)
    q_w = H * HD // (n_ctx * n_dp)
    p_w = KVH * HD // n_dp
    in_rows = q_w == HD and p_w == HD
    place = lax.axis_index("ctx").astype(jnp.int32).reshape(1)

    def move(array, chip, cross):
        pairs = [(i, (i + CORES * chip) % n_ctx ^ cross) for i in range(n_ctx)]
        return lax.ppermute(array, "ctx", pairs)

    mine, other = split_kv(place, key_in, value_in)
    pieces = [
        [mine[n]] + [move((mine, other)[x][n], s, x) for s, x in hops]
        for n in range(len(chunks))
    ]
    own, sends = weigh(place, masked, bucket, query, out_grad)
    swaps = [move(send, 0, 1) for send in sends]
    groups = returns_of(docs)
    near_q, far_q, near_kv, back_kv, sums, carry = [], [], [], [], [], []
    for n, (d, lo, hi) in enumerate(chunks):
        before = sums if in_rows and n == len(chunks) - 1 else []
        ranges = [chunk[1:] for chunk in chunks[:n]]
        (dq, dq_sib), sums_n, near, far, share = attend(
            place, own[d], swaps[d], pieces[n], lo, hi, carry, before, ranges, n_dp, n_ctx * n_dp
        )
        near_q.append(dq)
        near_kv.append(near)
        sums = sums + [sums_n]
        i = place_of(n, docs)[0]
        if n < groups[i][-1]:
            carry = [dq_sib, *far]
            continue
        carry = []
        back_kv.append([move(part, -s, x) for (s, x), part in zip(hops, far)])
        far_q.append(move(dq_sib, 0, 1))

    if not in_rows:
        share = shares_of(place, sums, chunks, n_ctx, n_dp)
    gathered = lax.all_to_all(share, ("ctx", "dp"), 0, 0)
    norm_factor = 1.0 / math.sqrt(docs * n_dp * tok * n_ctx)
    key_grad, value_grad = join_kv(place, near_kv, back_kv, docs, chips)
    query_grad = join_q(place, near_q, far_q, docs)
    bias_q, bias_kv = bias_out(gathered, norm_factor, q_w, p_w)
    return query_grad, key_grad, value_grad, bias_q, bias_kv


def solution(mesh):
    in_specs = (
        P("dp", "ctx", None),
        P("dp", "ctx", None),
        P("dp", "ctx", None),
        P("dp", "ctx", None),
        P("dp", None),
        P("dp", "ctx"),
    )
    out_specs = (
        P("dp", "ctx", None),
        P("dp", "ctx", None),
        P("dp", "ctx", None),
        P("ctx", "dp"),
        P(None, "dp"),
    )
    return jax.shard_map(
        step_device, mesh=mesh, in_specs=in_specs, out_specs=out_specs, check_vma=False
    )
```

time: 47.5 us -> 50.6 us (1.065)
  Pallas kernels: 7.94 us -> 11.4 us
  local copies, waits for them, and re-layouts: 3.21 us -> 0.68 us
  waiting for transfers between devices: 9.77 us -> 10.8 us
  starting transfers between devices: 13.7 us -> 14.4 us
    unnamed x12 -> x4, local copies, waits for them, and re-layouts: 3.21 us -> 0.68 us
    pallas_call x6, Pallas kernels: 6.59 us -> 8.54 us  [the longest x3 5.89 us: attend(): pl.pallas_call(functools.partial(attend_kernel, n_pieces, tok, lo, hi, sk...]
    pallas_call x1, Pallas kernels: 0.3 us -> 1.86 us  [weigh(): pl.pallas_call(weigh_kernel, grid_spec=pltpu.PrefetchScalarGridSpec(num_s...]
    ppermute x16 -> x19, waiting for transfers between devices: 9.77 us -> 10.8 us  [move(): return lax.ppermute(array, 'ctx', pairs)]
    ppermute x16 -> x19, starting transfers between devices: 13.7 us -> 14.4 us  [move(): return lax.ppermute(array, 'ctx', pairs)]
  transfers between devices with their start and end apart: 16 -> 19, of which waited for: 5 -> 7; matrix products, arithmetic and copies ran while one was open for 0% -> 0% of each run, Pallas kernels for 9% -> 14%
where the time goes in v3:
time: 50.6 us; the launch traced here: 50.3 us
  starting transfers between devices  14.4 us (28%)
  blocking collectives  12.3 us (24%)
  Pallas kernels  11.4 us (23%)
  waiting for transfers between devices  10.8 us (21%)
  between operations  0.72 us (1%)
  local copies, waits for them, and re-layouts  0.68 us (1%)
    ppermute x19, starting transfers between devices, move(): return lax.ppermute(array, 'ctx', pairs)  14.4 us
    all_to_all x1, blocking collectives, step_device(): gathered = lax.all_to_all(share, ('ctx', 'dp'), 0, 0)  12.3 us
    ppermute x19, waiting for transfers between devices, move(): return lax.ppermute(array, 'ctx', pairs)  10.8 us
    pallas_call x3, Pallas kernels, attend(): pl.pallas_call(functools.partial(attend_kernel, n_pieces, tok, lo, hi, sk...  5.89 us
    pallas_call x1, Pallas kernels, weigh(): pl.pallas_call(weigh_kernel, grid_spec=pltpu.PrefetchScalarGridSpec(num_s...  1.86 us
    pallas_call x1, Pallas kernels, split_kv(): pl.pallas_call(functools.partial(split_kv_kernel, chunks), in_specs=[IN_S...  1.1 us
    pallas_call x1, Pallas kernels, join_q(): pl.pallas_call(functools.partial(join_q_kernel, docs), in_specs=[IN_SMEM]...  1.05 us
  transfers between devices with their start and end apart: 19, of which 7 were waited for; matrix products, arithmetic and copies ran while one was open for 0% of the time, Pallas kernels for 14%

profile of v3, /device:TPU:0, one launch (start us, length us, event | category | flops | bytes accessed | tf_op | source)
XLA Modules:
  0.0 50.3 jit_solution(13408439703021149549)
XLA Ops:
  0.6 0.0 copy-start.1
  0.6 0.0 copy-start
  0.7 0.7 %copy-done.1 = s32[2,64]{1,0:T(2,128)S(1)} copy-done((s32[2,64]{1,0:T(2,128)S(1)}, s32[2,64]{1,0:T(2,128)}, u32[]{:S(2)}) %copy-start.1) | copy-done | bytes 536
  1.3 0.0 copy-done
  1.3 1.9 %weigh.1 = (bf16[2,64,2048]{2,1,0:T(8,128)(2,1)S(1)}, bf16[2,64,2048]{2,1,0:T(8,128)(2,1)S(1)}, bf16[2,64,2048]{2,1,0:T(8,128)(2,1)S(1)}, bf16[2,64,2048]{2,1,0:T(8,128)(2,1)S(1)}) custom-call(s32[1]{0:T(128)} %bitcast.place_ref, s32[2,128]{1,0:T(2,128)S(1)} %copy-done, s32[2,64]{1,0:T(2,128)S(1)} %copy-done.1, bf16[2,64,4096]{2,1,0:T(8,128)(2,1)} %query_ref.1, ...), custom_call_target="tpu_custom_call" | custom-call | tf_op jit(solution)/shard_map/weigh/pallas_call | solution.py:142
  3.2 0.6 %collective-permute-start = (bf16[2,64,2048]{2,1,0:T(8,128)(2,1)S(1)}, bf16[2,64,2048]{2,1,0:T(8,128)(2,1)S(1)}, u32[]{:S(2)}, u32[]{:S(2)}) collective-permute-start(bf16[2,64,2048]{2,1,0:T(8,128)(2,1)S(1)} %get-tuple-element.43), channel_id=1, source_target_pairs={{0,1},{1,0},{2,3},{3,2},{4,5},{5,4},{6,7},{7,6},{8,9},{9,8},{10,11... | collective-permute-start | bytes 1572872 | tf_op jit(solution)/shard_map/ppermute | solution.py:388
  3.7 0.1 collective-permute-start.4
  3.8 1.1 %split_kv.1 = (bf16[2,64,512]{2,1,0:T(8,128)(2,1)S(1)}, bf16[2,64,512]{2,1,0:T(8,128)(2,1)S(1)}, bf16[2,64,256]{2,1,0:T(8,128)(2,1)S(1)}, bf16[2,64,256]{2,1,0:T...) custom-call(s32[1]{0:T(128)} %bitcast.place_ref, bf16[2,64,1024]{2,1,0:T(8,128)(2,1)} %key_ref.1, ...), custom_call_target="tpu_custom_call" | custom-call | tf_op jit(solution)/shard_map/split_kv/pallas_call | solution.py:107
  4.9 3.0 %collective-permute-start.1 = (bf16[2,64,512]{2,1,0:T(8,128)(2,1)S(1)}, bf16[2,64,512]{2,1,0:T(8,128)(2,1)S(1)}, u32[]{:S(2)}, u32[]{:S(2)}) collective-permute-start(bf16[2,64,512]{2,1,0:T(8,128)(2,1)S(1)} %get-tuple-element.44.refs_0_), channel_id=1, source_target_pairs={{0,2},{1,3},{2,0},{3,1},{4,6},{5,7},{6,4},{7,5},{8,10},{9,11},{10,... | collective-permute-start | bytes 393224 | tf_op jit(solution)/shard_map/ppermute | solution.py:388
  7.9 0.0 collective-permute-start.2
  7.9 0.2 collective-permute-start.3
  8.1 4.2 %collective-permute-done.1.refs_1_ = bf16[2,64,512]{2,1,0:T(8,128)(2,1)S(1)} collective-permute-done((bf16[2,64,512]{2,1,0:T(8,128)(2,1)S(1)}, bf16[2,64,512]{2,1,0:T(8,128)(2,1)S(1)}, u32[]{:S(2)}, u32[]{:S(2)}) %collective-permute-start.1) | collective-permute-done | bytes 131104 | tf_op jit(solution)/shard_map/ppermute | solution.py:388
  12.3 2.0 %collective-permute-start.5 = (bf16[2,64,256]{2,1,0:T(8,128)(2,1)S(1)}, bf16[2,64,256]{2,1,0:T(8,128)(2,1)S(1)}, u32[]{:S(2)}, u32[]{:S(2)}) collective-permute-start(bf16[2,64,256]{2,1,0:T(8,128)(2,1)S(1)} %get-tuple-element.49.refs_0_), channel_id=1, source_target_pairs={{0,2},{1,3},{2,0},{3,1},{4,6},{5,7},{6,4},{7,5},{8,10},{9,11},{10,... | collective-permute-start | bytes 196616 | tf_op jit(solution)/shard_map/ppermute | solution.py:388
  14.3 0.1 collective-permute-done.2.refs_2_
  14.4 1.9 %collective-permute-start.6 = (bf16[2,64,256]{2,1,0:T(8,128)(2,1)S(1)}, bf16[2,64,256]{2,1,0:T(8,128)(2,1)S(1)}, u32[]{:S(2)}, u32[]{:S(2)}) collective-permute-start(bf16[2,64,256]{2,1,0:T(8,128)(2,1)S(1)} %get-tuple-element.50), channel_id=1, source_target_pairs={{0,3},{1,2},{2,1},{3,0},{4,7},{5,6},{6,5},{7,4},{8,11},{9,10},{10,... | collective-permute-start | bytes 196616 | tf_op jit(solution)/shard_map/ppermute | solution.py:388
  16.4 0.0 collective-permute-done.3.refs_3_
  16.4 0.0 collective-permute-start.7
  16.4 0.0 collective-permute-done.swap_ref
  16.4 2.5 %attend.3 = (bf16[64,2048]{1,0:T(8,128)(2,1)S(1)}, bf16[64,2048]{1,0:T(8,128)(2,1)S(1)}, f32[16,128]{1,0:T(8,128)S(1)}, f32[4,256]{1,0:T(4,128)S(1)}, f32[2,64,5...) custom-call(s32[1]{0:T(128)} %bitcast.place_ref, ...), custom_call_target="tpu_custom_call" | custom-call | tf_op jit(solution)/shard_map/attend/pallas_call | solution.py:241
  18.9 0.0 collective-permute-done.5.refs_1_
  18.9 0.0 collective-permute-done.6.refs_2_
  18.9 0.0 collective-permute-done.7.refs_3_
  18.9 0.0 collective-permute-done.4.swap_ref
  18.9 1.4 %attend.4 = (bf16[64,1024]{1,0:T(8,128)(2,1)S(1)}, bf16[64,3072]{1,0:T(8,128)(2,1)S(1)}, f32[8,128]{1,0:T(8,128)S(1)}, f32[2,256]{1,0:T(2,128)S(1)}, f32[2,64,25...) custom-call(s32[1]{0:T(128)} %bitcast.place_ref, ...), custom_call_target="tpu_custom_call" | custom-call | tf_op jit(solution)/shard_map/attend/pallas_call | solution.py:241
  20.3 0.6 %collective-permute-start.11 = (bf16[64,3072]{1,0:T(8,128)(2,1)S(1)}, bf16[64,3072]{1,0:T(8,128)(2,1)S(1)}, u32[]{:S(2)}, u32[]{:S(2)}) collective-permute-start(bf16[64,3072]{1,0:T(8,128)(2,1)S(1)} %get-tuple-element.63), channel_id=1, source_target_pairs={{0,1},{1,0},{2,3},{3,2},{4,5},{5,4},{6,7},{7,6},{8,9},{9,8},{10,11... | collective-permute-start | bytes 1179656 | tf_op jit(solution)/shard_map/ppermute | solution.py:388
  20.9 0.1 collective-permute-start.10
  21.0 1.0 %collective-permute-start.8 = (bf16[2,64,256]{2,1,0:T(8,128)(2,1)S(1)}, bf16[2,64,256]{2,1,0:T(8,128)(2,1)S(1)}, u32[]{:S(2)}, u32[]{:S(2)}) collective-permute-start(bf16[2,64,256]{2,1,0:T(8,128)(2,1)S(1)} %get-tuple-element.56.refs_0_), channel_id=1, source_target_pairs={{0,2},{1,3},{2,0},{3,1},{4,6},{5,7},{6,4},{7,5},{8,10},{9,11},{10,... | collective-permute-start | bytes 196616 | tf_op jit(solution)/shard_map/ppermute | solution.py:388
  22.0 0.8 %collective-permute-start.9 = (bf16[2,64,256]{2,1,0:T(8,128)(2,1)S(1)}, bf16[2,64,256]{2,1,0:T(8,128)(2,1)S(1)}, u32[]{:S(2)}, u32[]{:S(2)}) collective-permute-start(bf16[2,64,256]{2,1,0:T(8,128)(2,1)S(1)} %get-tuple-element.57), channel_id=1, source_target_pairs={{0,3},{1,2},{2,1},{3,0},{4,7},{5,6},{6,5},{7,4},{8,11},{9,10},{10,... | collective-permute-start | bytes 196616 | tf_op jit(solution)/shard_map/ppermute | solution.py:388
  22.8 0.0 collective-permute-done.10.refs_3_
  22.8 3.1 %collective-permute-done.8.refs_1_ = bf16[2,64,256]{2,1,0:T(8,128)(2,1)S(1)} collective-permute-done((bf16[2,64,256]{2,1,0:T(8,128)(2,1)S(1)}, bf16[2,64,256]{2,1,0:T(8,128)(2,1)S(1)}, u32[]{:S(2)}, u32[]{:S(2)}) %collective-permute-start.8) | collective-permute-done | bytes 65568 | tf_op jit(solution)/shard_map/ppermute | solution.py:388
  25.8 0.6 %collective-permute-done.9.refs_2_ = bf16[2,64,256]{2,1,0:T(8,128)(2,1)S(1)} collective-permute-done((bf16[2,64,256]{2,1,0:T(8,128)(2,1)S(1)}, bf16[2,64,256]{2,1,0:T(8,128)(2,1)S(1)}, u32[]{:S(2)}, u32[]{:S(2)}) %collective-permute-start.9) | collective-permute-done | bytes 65568 | tf_op jit(solution)/shard_map/ppermute | solution.py:388
  26.4 2.0 %attend.5 = (bf16[64,1024]{1,0:T(8,128)(2,1)S(1)}, bf16[64,1024]{1,0:T(8,128)(2,1)S(1)}, f32[8,128]{1,0:T(8,128)}, f32[2,256]{1,0:T(2,128)}, f32[2,64,256]{2,1,0...) custom-call(s32[1]{0:T(128)} %bitcast.place_ref, ...), custom_call_target="tpu_custom_call" | custom-call | tf_op jit(solution)/shard_map/attend/pallas_call | solution.py:241
  28.4 1.0 %collective-permute-start.16 = (bf16[2,64,256]{2,1,0:T(8,128)(2,1)S(1)}, bf16[2,64,256]{2,1,0:T(8,128)(2,1)S(1)}, u32[]{:S(2)}, u32[]{:S(2)}) collective-permute-start(bf16[2,64,256]{2,1,0:T(8,128)(2,1)S(1)} %get-tuple-element.71), channel_id=1, source_target_pairs={{0,2},{1,3},{2,0},{3,1},{4,6},{5,7},{6,4},{7,5},{8,10},{9,11},{10,... | collective-permute-start | bytes 196616 | tf_op jit(solution)/shard_map/ppermute | solution.py:388
  29.4 0.6 %collective-permute-start.17 = (bf16[2,64,256]{2,1,0:T(8,128)(2,1)S(1)}, bf16[2,64,256]{2,1,0:T(8,128)(2,1)S(1)}, u32[]{:S(2)}, u32[]{:S(2)}) collective-permute-start(bf16[2,64,256]{2,1,0:T(8,128)(2,1)S(1)} %get-tuple-element.72), channel_id=1, source_target_pairs={{0,3},{1,2},{2,1},{3,0},{4,7},{5,6},{6,5},{7,4},{8,11},{9,10},{10,... | collective-permute-start | bytes 196616 | tf_op jit(solution)/shard_map/ppermute | solution.py:388
  29.9 1.0 %collective-permute-start.13 = (bf16[2,64,768]{2,1,0:T(8,128)(2,1)S(1)}, bf16[2,64,768]{2,1,0:T(8,128)(2,1)S(1)}, u32[]{:S(2)}, u32[]{:S(2)}) collective-permute-start(bf16[2,64,768]{2,1,0:T(8,128)(2,1)S(1)} %get-tuple-element.68), channel_id=1, source_target_pairs={{0,2},{1,3},{2,0},{3,1},{4,6},{5,7},{6,4},{7,5},{8,10},{9,11},{10,... | collective-permute-start | bytes 589832 | tf_op jit(solution)/shard_map/ppermute | solution.py:388
  31.0 0.9 %collective-permute-start.14 = (bf16[2,64,768]{2,1,0:T(8,128)(2,1)S(1)}, bf16[2,64,768]{2,1,0:T(8,128)(2,1)S(1)}, u32[]{:S(2)}, u32[]{:S(2)}) collective-permute-start(bf16[2,64,768]{2,1,0:T(8,128)(2,1)S(1)} %get-tuple-element.69), channel_id=1, source_target_pairs={{0,3},{1,2},{2,1},{3,0},{4,7},{5,6},{6,5},{7,4},{8,11},{9,10},{10,... | collective-permute-start | bytes 589832 | tf_op jit(solution)/shard_map/ppermute | solution.py:388
  31.9 1.0 %collective-permute-done.16.refs_6_ = bf16[2,64,256]{2,1,0:T(8,128)(2,1)S(1)} collective-permute-done((bf16[2,64,256]{2,1,0:T(8,128)(2,1)S(1)}, bf16[2,64,256]{2,1,0:T(8,128)(2,1)S(1)}, u32[]{:S(2)}, u32[]{:S(2)}) %collective-permute-start.16) | collective-permute-done | bytes 65568 | tf_op jit(solution)/shard_map/ppermute | solution.py:388
  32.9 0.0 collective-permute-start.15
  32.9 0.9 %collective-permute-done.17.refs_7_ = bf16[2,64,256]{2,1,0:T(8,128)(2,1)S(1)} collective-permute-done((bf16[2,64,256]{2,1,0:T(8,128)(2,1)S(1)}, bf16[2,64,256]{2,1,0:T(8,128)(2,1)S(1)}, u32[]{:S(2)}, u32[]{:S(2)}) %collective-permute-start.17) | collective-permute-done | bytes 65568 | tf_op jit(solution)/shard_map/ppermute | solution.py:388
  33.8 0.4 collective-permute-start.18
  34.1 0.9 %collective-permute-done.18.refs_8_ = bf16[2,64,256]{2,1,0:T(8,128)(2,1)S(1)} collective-permute-done((bf16[2,64,256]{2,1,0:T(8,128)(2,1)S(1)}, bf16[2,64,256]{2,1,0:T(8,128)(2,1)S(1)}, u32[]{:S(2)}, u32[]{:S(2)}) %collective-permute-start.18) | collective-permute-done | bytes 65568 | tf_op jit(solution)/shard_map/ppermute | solution.py:388
  35.0 0.4 collective-permute-start.12
  35.4 12.3 %all_to_all.5.gathered_ref = f32[32,1,384]{2,1,0:T(1,128)S(1)} all-to-all(f32[32,1,384]{2,1,0:T(1,128)S(1)} %get-tuple-element.76), channel_id=1, replica_groups=mesh['dp'=8,'ctx'=4] {'ctx','dp'}, dimensions={0} | all-to-all | bytes 98304 | tf_op jit(solution)/shard_map/all_to_all | solution.py:418
  47.7 0.6 %bias_out.1 = (f32[1,128]{1,0:T(1,128)}, f32[2,128]{1,0:T(2,128)}) custom-call(f32[32,1,384]{2,1,0:T(1,128)S(1)} %all_to_all.5.gathered_ref), custom_call_target="tpu_custom_call" | custom-call | tf_op jit(solution)/shard_map/bias_out/pallas_call | solution.py:358
  48.3 0.0 collective-permute-done.13.refs_3_
  48.3 0.0 collective-permute-done.14.refs_4_
  48.3 0.0 collective-permute-done.15.refs_5_
  48.3 0.9 %join_kv.1 = (bf16[2,64,1024]{2,1,0:T(8,128)(2,1)}, bf16[2,64,1024]{2,1,0:T(8,128)(2,1)}) custom-call(s32[1]{0:T(128)} %bitcast.place_ref, f32[2,64,512]{2,1,0:T(8,128)S(1)} %get-tuple-element.65.refs_0_, f32[2,64,256]{2,1,0:T(8,128)S(1)} %get-tuple-element.66.refs_1_, f32[2,64,256]{2,1,0:T(8,128)S(1)} %get-tuple-element.67.refs_2_, ...), custom_call_target="tpu_custom_call" | custom-call | tf_op jit(solution)/shard_map/join_kv/pallas_call | solution.py:340
  49.3 0.0 collective-permute-done.12.refs_4_
  49.3 0.0 collective-permute-done.11.refs_3_
  49.3 1.0 %join_q.1 = bf16[2,64,4096]{2,1,0:T(8,128)(2,1)} custom-call(s32[1]{0:T(128)} %bitcast.place_ref, bf16[64,2048]{1,0:T(8,128)(2,1)S(1)} %get-tuple-element.46.refs_0_, bf16[64,1024]{1,0:T(8,128)(2,1)S(1)} %get-tuple-element.55.refs_1_, bf16[64,1024]{1,0:T(8,128)(2,1)S(1)} %get-tuple-element.62.refs_2_, bf16[64,3072]{1,0:T(8,128)(2,1)S(1)} %collective-permute-done.11.refs_3_, ...), custom_call_target="tpu_custom_call" | custom-call | tf_op jit(solution)/shard_map/join_q/pallas_call | solution.py:303
Async XLA Ops:
  0.6 0.7 %copy-start.1 = (s32[2,64]{1,0:T(2,128)S(1)}, s32[2,64]{1,0:T(2,128)}, u32[]{:S(2)}) copy-start(s32[2,64]{1,0:T(2,128)} %bucket_ref.1) | copy-start | bytes 1540
  0.6 0.7 %copy-start = (s32[2,128]{1,0:T(2,128)S(1)}, s32[2,128]{1,0:T(2,128)}, u32[]{:S(2)}) copy-start(s32[2,128]{1,0:T(2,128)} %masked_ref.1) | copy-start | bytes 3076
  3.2 13.2 %collective-permute-start = (bf16[2,64,2048]{2,1,0:T(8,128)(2,1)S(1)}, bf16[2,64,2048]{2,1,0:T(8,128)(2,1)S(1)}, u32[]{:S(2)}, u32[]{:S(2)}) collective-permute-start(bf16[2,64,2048]{2,1,0:T(8,128)(2,1)S(1)} %get-tuple-element.43), channel_id=1, source_target_pairs={{0,1},{1,0},{2,3},{3,2},{4,5},{5,4},{6,7},{7,6},{8,9},{9,8},{10,11... | collective-permute-start | bytes 1572872 | tf_op jit(solution)/shard_map/ppermute | solution.py:388
  3.7 15.2 %collective-permute-start.4 = (bf16[2,64,2048]{2,1,0:T(8,128)(2,1)S(1)}, bf16[2,64,2048]{2,1,0:T(8,128)(2,1)S(1)}, u32[]{:S(2)}, u32[]{:S(2)}) collective-permute-start(bf16[2,64,2048]{2,1,0:T(8,128)(2,1)S(1)} %get-tuple-element.48), channel_id=1, source_target_pairs={{0,1},{1,0},{2,3},{3,2},{4,5},{5,4},{6,7},{7,6},{8,9},{9,8},{10,11... | collective-permute-start | bytes 1572872 | tf_op jit(solution)/shard_map/ppermute | solution.py:388
  4.9 7.3 %collective-permute-start.1 = (bf16[2,64,512]{2,1,0:T(8,128)(2,1)S(1)}, bf16[2,64,512]{2,1,0:T(8,128)(2,1)S(1)}, u32[]{:S(2)}, u32[]{:S(2)}) collective-permute-start(bf16[2,64,512]{2,1,0:T(8,128)(2,1)S(1)} %get-tuple-element.44.refs_0_), channel_id=1, source_target_pairs={{0,2},{1,3},{2,0},{3,1},{4,6},{5,7},{6,4},{7,5},{8,10},{9,11},{10,... | collective-permute-start | bytes 393224 | tf_op jit(solution)/shard_map/ppermute | solution.py:388
  7.9 6.5 %collective-permute-start.2 = (bf16[2,64,512]{2,1,0:T(8,128)(2,1)S(1)}, bf16[2,64,512]{2,1,0:T(8,128)(2,1)S(1)}, u32[]{:S(2)}, u32[]{:S(2)}) collective-permute-start(bf16[2,64,512]{2,1,0:T(8,128)(2,1)S(1)} %get-tuple-element.45), channel_id=1, source_target_pairs={{0,3},{1,2},{2,1},{3,0},{4,7},{5,6},{6,5},{7,4},{8,11},{9,10},{10,... | collective-permute-start | bytes 393224 | tf_op jit(solution)/shard_map/ppermute | solution.py:388
  7.9 8.4 %collective-permute-start.3 = (bf16[2,64,512]{2,1,0:T(8,128)(2,1)S(1)}, bf16[2,64,512]{2,1,0:T(8,128)(2,1)S(1)}, u32[]{:S(2)}, u32[]{:S(2)}) collective-permute-start(bf16[2,64,512]{2,1,0:T(8,128)(2,1)S(1)} %get-tuple-element.45), channel_id=1, source_target_pairs={{0,1},{1,0},{2,3},{3,2},{4,5},{5,4},{6,7},{7,6},{8,9},{9,8},{10,11... | collective-permute-start | bytes 393224 | tf_op jit(solution)/shard_map/ppermute | solution.py:388
  12.3 6.6 %collective-permute-start.5 = (bf16[2,64,256]{2,1,0:T(8,128)(2,1)S(1)}, bf16[2,64,256]{2,1,0:T(8,128)(2,1)S(1)}, u32[]{:S(2)}, u32[]{:S(2)}) collective-permute-start(bf16[2,64,256]{2,1,0:T(8,128)(2,1)S(1)} %get-tuple-element.49.refs_0_), channel_id=1, source_target_pairs={{0,2},{1,3},{2,0},{3,1},{4,6},{5,7},{6,4},{7,5},{8,10},{9,11},{10,... | collective-permute-start | bytes 196616 | tf_op jit(solution)/shard_map/ppermute | solution.py:388
  14.4 4.4 %collective-permute-start.6 = (bf16[2,64,256]{2,1,0:T(8,128)(2,1)S(1)}, bf16[2,64,256]{2,1,0:T(8,128)(2,1)S(1)}, u32[]{:S(2)}, u32[]{:S(2)}) collective-permute-start(bf16[2,64,256]{2,1,0:T(8,128)(2,1)S(1)} %get-tuple-element.50), channel_id=1, source_target_pairs={{0,3},{1,2},{2,1},{3,0},{4,7},{5,6},{6,5},{7,4},{8,11},{9,10},{10,... | collective-permute-start | bytes 196616 | tf_op jit(solution)/shard_map/ppermute | solution.py:388
  16.4 2.5 %collective-permute-start.7 = (bf16[2,64,256]{2,1,0:T(8,128)(2,1)S(1)}, bf16[2,64,256]{2,1,0:T(8,128)(2,1)S(1)}, u32[]{:S(2)}, u32[]{:S(2)}) collective-permute-start(bf16[2,64,256]{2,1,0:T(8,128)(2,1)S(1)} %get-tuple-element.50), channel_id=1, source_target_pairs={{0,1},{1,0},{2,3},{3,2},{4,5},{5,4},{6,7},{7,6},{8,9},{9,8},{10,11... | collective-permute-start | bytes 196616 | tf_op jit(solution)/shard_map/ppermute | solution.py:388
  20.3 28.9 %collective-permute-start.11 = (bf16[64,3072]{1,0:T(8,128)(2,1)S(1)}, bf16[64,3072]{1,0:T(8,128)(2,1)S(1)}, u32[]{:S(2)}, u32[]{:S(2)}) collective-permute-start(bf16[64,3072]{1,0:T(8,128)(2,1)S(1)} %get-tuple-element.63), channel_id=1, source_target_pairs={{0,1},{1,0},{2,3},{3,2},{4,5},{5,4},{6,7},{7,6},{8,9},{9,8},{10,11... | collective-permute-start | bytes 1179656 | tf_op jit(solution)/shard_map/ppermute | solution.py:388
  20.9 1.9 %collective-permute-start.10 = (bf16[2,64,256]{2,1,0:T(8,128)(2,1)S(1)}, bf16[2,64,256]{2,1,0:T(8,128)(2,1)S(1)}, u32[]{:S(2)}, u32[]{:S(2)}) collective-permute-start(bf16[2,64,256]{2,1,0:T(8,128)(2,1)S(1)} %get-tuple-element.57), channel_id=1, source_target_pairs={{0,1},{1,0},{2,3},{3,2},{4,5},{5,4},{6,7},{7,6},{8,9},{9,8},{10,11... | collective-permute-start | bytes 196616 | tf_op jit(solution)/shard_map/ppermute | solution.py:388
  21.0 4.8 %collective-permute-start.8 = (bf16[2,64,256]{2,1,0:T(8,128)(2,1)S(1)}, bf16[2,64,256]{2,1,0:T(8,128)(2,1)S(1)}, u32[]{:S(2)}, u32[]{:S(2)}) collective-permute-start(bf16[2,64,256]{2,1,0:T(8,128)(2,1)S(1)} %get-tuple-element.56.refs_0_), channel_id=1, source_target_pairs={{0,2},{1,3},{2,0},{3,1},{4,6},{5,7},{6,4},{7,5},{8,10},{9,11},{10,... | collective-permute-start | bytes 196616 | tf_op jit(solution)/shard_map/ppermute | solution.py:388
  22.0 4.4 %collective-permute-start.9 = (bf16[2,64,256]{2,1,0:T(8,128)(2,1)S(1)}, bf16[2,64,256]{2,1,0:T(8,128)(2,1)S(1)}, u32[]{:S(2)}, u32[]{:S(2)}) collective-permute-start(bf16[2,64,256]{2,1,0:T(8,128)(2,1)S(1)} %get-tuple-element.57), channel_id=1, source_target_pairs={{0,3},{1,2},{2,1},{3,0},{4,7},{5,6},{6,5},{7,4},{8,11},{9,10},{10,... | collective-permute-start | bytes 196616 | tf_op jit(solution)/shard_map/ppermute | solution.py:388
  28.4 4.5 %collective-permute-start.16 = (bf16[2,64,256]{2,1,0:T(8,128)(2,1)S(1)}, bf16[2,64,256]{2,1,0:T(8,128)(2,1)S(1)}, u32[]{:S(2)}, u32[]{:S(2)}) collective-permute-start(bf16[2,64,256]{2,1,0:T(8,128)(2,1)S(1)} %get-tuple-element.71), channel_id=1, source_target_pairs={{0,2},{1,3},{2,0},{3,1},{4,6},{5,7},{6,4},{7,5},{8,10},{9,11},{10,... | collective-permute-start | bytes 196616 | tf_op jit(solution)/shard_map/ppermute | solution.py:388
  29.4 4.4 %collective-permute-start.17 = (bf16[2,64,256]{2,1,0:T(8,128)(2,1)S(1)}, bf16[2,64,256]{2,1,0:T(8,128)(2,1)S(1)}, u32[]{:S(2)}, u32[]{:S(2)}) collective-permute-start(bf16[2,64,256]{2,1,0:T(8,128)(2,1)S(1)} %get-tuple-element.72), channel_id=1, source_target_pairs={{0,3},{1,2},{2,1},{3,0},{4,7},{5,6},{6,5},{7,4},{8,11},{9,10},{10,... | collective-permute-start | bytes 196616 | tf_op jit(solution)/shard_map/ppermute | solution.py:388
  29.9 18.4 %collective-permute-start.13 = (bf16[2,64,768]{2,1,0:T(8,128)(2,1)S(1)}, bf16[2,64,768]{2,1,0:T(8,128)(2,1)S(1)}, u32[]{:S(2)}, u32[]{:S(2)}) collective-permute-start(bf16[2,64,768]{2,1,0:T(8,128)(2,1)S(1)} %get-tuple-element.68), channel_id=1, source_target_pairs={{0,2},{1,3},{2,0},{3,1},{4,6},{5,7},{6,4},{7,5},{8,10},{9,11},{10,... | collective-permute-start | bytes 589832 | tf_op jit(solution)/shard_map/ppermute | solution.py:388
  31.0 17.4 %collective-permute-start.14 = (bf16[2,64,768]{2,1,0:T(8,128)(2,1)S(1)}, bf16[2,64,768]{2,1,0:T(8,128)(2,1)S(1)}, u32[]{:S(2)}, u32[]{:S(2)}) collective-permute-start(bf16[2,64,768]{2,1,0:T(8,128)(2,1)S(1)} %get-tuple-element.69), channel_id=1, source_target_pairs={{0,3},{1,2},{2,1},{3,0},{4,7},{5,6},{6,5},{7,4},{8,11},{9,10},{10,... | collective-permute-start | bytes 589832 | tf_op jit(solution)/shard_map/ppermute | solution.py:388
  32.9 15.4 %collective-permute-start.15 = (bf16[2,64,768]{2,1,0:T(8,128)(2,1)S(1)}, bf16[2,64,768]{2,1,0:T(8,128)(2,1)S(1)}, u32[]{:S(2)}, u32[]{:S(2)}) collective-permute-start(bf16[2,64,768]{2,1,0:T(8,128)(2,1)S(1)} %get-tuple-element.70), channel_id=1, source_target_pairs={{0,1},{1,0},{2,3},{3,2},{4,5},{5,4},{6,7},{7,6},{8,9},{9,8},{10,11... | collective-permute-start | bytes 589832 | tf_op jit(solution)/shard_map/ppermute | solution.py:388
  33.8 1.3 %collective-permute-start.18 = (bf16[2,64,256]{2,1,0:T(8,128)(2,1)S(1)}, bf16[2,64,256]{2,1,0:T(8,128)(2,1)S(1)}, u32[]{:S(2)}, u32[]{:S(2)}) collective-permute-start(bf16[2,64,256]{2,1,0:T(8,128)(2,1)S(1)} %get-tuple-element.73), channel_id=1, source_target_pairs={{0,1},{1,0},{2,3},{3,2},{4,5},{5,4},{6,7},{7,6},{8,9},{9,8},{10,11... | collective-permute-start | bytes 196616 | tf_op jit(solution)/shard_map/ppermute | solution.py:388
  35.0 14.2 %collective-permute-start.12 = (bf16[64,1024]{1,0:T(8,128)(2,1)S(1)}, bf16[64,1024]{1,0:T(8,128)(2,1)S(1)}, u32[]{:S(2)}, u32[]{:S(2)}) collective-permute-start(bf16[64,1024]{1,0:T(8,128)(2,1)S(1)} %get-tuple-element.64), channel_id=1, source_target_pairs={{0,1},{1,0},{2,3},{3,2},{4,5},{5,4},{6,7},{7,6},{8,9},{9,8},{10,11... | collective-permute-start | bytes 393224 | tf_op jit(solution)/shard_map/ppermute | solution.py:388
